TPU v7x, 512 devices: a whole 4x8x8 slice. The times are simulated.
512 devices in a mesh: slab: 32 (over y, x_lo, core), space: 16 (over x_hi, z).
Axes of the slice: x: 4 (x_hi: 2, x_lo: 2; x = x_hi * 2 + x_lo), y: 8, z: 8, core: 2. Of those that a mesh axis runs over, the one named last changes fastest.
Arguments:
- query_rows: bfloat16 [131072, 128], P(('slab', 'space')), may hold values from -4 to 4, as said below
- key_rows: bfloat16 [131072, 128], P(('slab', 'space')), may hold values from -4 to 4, as said below
- value_rows: bfloat16 [131072, 128], P(('slab', 'space')), may hold values from -6 to 6
- out_saved: bfloat16 [131072, 128], P(('slab', 'space')), may hold values from -1.796875 to 1.796875
- grad_out: bfloat16 [131072, 128], P(('slab', 'space')), may hold values from -6 to 6
- log_norm: float32 [1, 131072], P(None, ('slab', 'space')), as said below
- band_mask: int32 [6, 32, 32], replicated, may hold values from 0 to 1, as said below
- frame_of_slab: int32 [32], replicated, may hold values from 0 to 31, as said below
Outputs:
- grad_query: bfloat16 [131072, 128], P(('slab', 'space'))
- grad_key: bfloat16 [131072, 128], P(('slab', 'space'))
- grad_value: bfloat16 [131072, 128], P(('slab', 'space'))
Inputs may be any that keep to these rules, and one draw needn't show every extreme that they name: query_rows are drawn afresh for each token. key_rows are drawn afresh for each token. log_norm[h, t] is the log of the sum over u with allowed[t, u] = 1 of exp(q_h(t) . k_h(u) / sqrt(128)) for the given queries and keys. band_mask[0, a, b] = 1 whenever tiles a and b differ by at most 1; band_mask[0, a, b] is 0 unless a // 2 and b // 2 differ by at most 1; for levels 1 and up, band_mask[l, a, b] is 0 unless a // 2 and b // 2 are equal. frame_of_slab names every frame once.
All inputs are finite; a program needn't handle non-finite values.
Results may differ from a plain program's by a relative error of at most 0.0075.
Values may be sent and summed in bfloat16 or wider, within the bound.
A program may use at most 64 MiB of HBM per device.

v0:
```python
import jax
import jax.numpy as jnp
from jax import lax
from jax.sharding import PartitionSpec as P

TILE = 128


def passed_along(block, axis, distance):
    devices = range(lax.axis_size(axis))
    route = [((i - distance) % len(devices), i) for i in devices]
    return lax.ppermute(block, axis, route)


def padded(block, sides, width):
    for axis, dim in sides:
        count = lax.axis_size(axis)
        forward = [(i, i + 1) for i in range(count - 1)]
        backward = [(target, source) for source, target in forward]
        low = lax.ppermute(
            lax.slice_in_dim(block, block.shape[dim] - width, None, axis=dim), axis, forward
        )
        high = lax.ppermute(lax.slice_in_dim(block, 0, width, axis=dim), axis, backward)
        block = jnp.concatenate([low, block, high], axis=dim)
    return block


def shifted(value, axis, by):
    length = lax.axis_size(axis)
    pairs = [(i, i + by) for i in range(length) if 0 <= i + by < length]
    return lax.ppermute(value, axis, pairs)


def expand_tiles(tile_mask):
    return jnp.repeat(jnp.repeat(tile_mask, TILE, axis=-2), TILE, axis=-1) > 0


def level_of(distance, level_count):
    powers = jnp.left_shift(jnp.int32(1), jnp.arange(level_count - 1, dtype=jnp.int32))
    return jnp.sum((distance >= powers).astype(jnp.int32))


def split_heads(rows, head_count):
    return rows.reshape(rows.shape[0], head_count, -1)


def probs_of(query3, key3, log_norm, allow):
    score_scale = query3.shape[2] ** (-0.5)
    scores = (
        jnp.einsum("qhd,khd->hqk", query3, key3, preferred_element_type=jnp.float32) * score_scale
    )
    return jnp.where(allow[None], jnp.exp(scores - log_norm[:, :, None]), 0.0)


def score_grads(query, grad_rows, log_norm, delta, key_block, value_block, allow):
    head_count = log_norm.shape[0]
    query3 = split_heads(query, head_count)
    grad3 = split_heads(grad_rows, head_count)
    key3 = split_heads(key_block, head_count)
    value3 = split_heads(value_block, head_count)
    prob = probs_of(query3, key3, log_norm, allow)
    dprob = jnp.einsum("qhd,khd->hqk", grad3, value3, preferred_element_type=jnp.float32)
    dscore = prob * (dprob - delta[:, :, None])
    return (query3, grad3, key3, prob, dscore)


def query_side(query, grad_rows, log_norm, delta, key_block, value_block, allow):
    query3, grad3, key3, prob, dscore = score_grads(
        query, grad_rows, log_norm, delta, key_block, value_block, allow
    )
    score_scale = query3.shape[2] ** (-0.5)
    grad_query = jnp.einsum(
        "hqk,khd->qhd", dscore.astype(jnp.bfloat16), key3, preferred_element_type=jnp.float32
    )
    return grad_query.reshape(query.shape[0], -1) * score_scale


def key_side(query, grad_rows, log_norm, delta, key_block, value_block, allow):
    query3, grad3, key3, prob, dscore = score_grads(
        query, grad_rows, log_norm, delta, key_block, value_block, allow
    )
    score_scale = query3.shape[2] ** (-0.5)
    key_count = key_block.shape[0]
    grad_key = jnp.einsum(
        "hqk,qhd->khd", dscore.astype(jnp.bfloat16), query3, preferred_element_type=jnp.float32
    )
    grad_value = jnp.einsum(
        "hqk,qhd->khd", prob.astype(jnp.bfloat16), grad3, preferred_element_type=jnp.float32
    )
    return jnp.stack(
        [grad_key.reshape(key_count, -1) * score_scale, grad_value.reshape(key_count, -1)]
    )


def full_grads(query, grad_rows, log_norm, delta, key_block, value_block, allow):
    query3, grad3, key3, prob, dscore = score_grads(
        query, grad_rows, log_norm, delta, key_block, value_block, allow
    )
    score_scale = query3.shape[2] ** (-0.5)
    key_count = key_block.shape[0]
    score_half = dscore.astype(jnp.bfloat16)
    grad_query = jnp.einsum("hqk,khd->qhd", score_half, key3, preferred_element_type=jnp.float32)
    grad_key = jnp.einsum("hqk,qhd->khd", score_half, query3, preferred_element_type=jnp.float32)
    grad_value = jnp.einsum(
        "hqk,qhd->khd", prob.astype(jnp.bfloat16), grad3, preferred_element_type=jnp.float32
    )
    pair_grads = jnp.stack(
        [grad_key.reshape(key_count, -1) * score_scale, grad_value.reshape(key_count, -1)]
    )
    return (grad_query.reshape(query.shape[0], -1) * score_scale, pair_grads)


def pass_keys(pair):
    return passed_along(pair, "slab", 1)


def body(query_rows, key_rows, value_rows, out_saved, grad_out, log_norm, band_mask, frame_of_slab):
    local_rows = query_rows.shape[0]
    width = query_rows.shape[1]
    head_count = log_norm.shape[0]
    per_device = local_rows // TILE
    level_count = band_mask.shape[0]
    slab_count = lax.axis_size("slab")
    slab_index = lax.axis_index("slab")
    column = lax.axis_index("space")
    product = grad_out.astype(jnp.float32) * out_saved.astype(jnp.float32)
    delta = product.reshape(local_rows, head_count, -1).sum(-1).T
    padded_mask = jnp.pad(band_mask[0], ((0, 0), (per_device, per_device)))
    start = column * per_device
    window_tiles = lax.dynamic_slice(padded_mask, (start, start), (per_device, 3 * per_device))
    window_allow = expand_tiles(window_tiles)
    key_pair = jnp.stack([key_rows, value_rows])
    wide_pair = padded(key_pair, (("space", 1),), local_rows)
    win_q, wide_grads = full_grads(
        query_rows, grad_out, log_norm, delta, wide_pair[0], wide_pair[1], window_allow
    )
    from_lower = shifted(wide_grads[:, 2 * local_rows :], "space", 1)
    from_upper = shifted(wide_grads[:, :local_rows], "space", -1)
    own_grads = wide_grads[:, local_rows : 2 * local_rows] + from_lower + from_upper
    level_tiles = lax.dynamic_slice(
        band_mask, (0, start, start), (level_count, per_device, per_device)
    )
    level_allow = expand_tiles(level_tiles)
    own_frame = frame_of_slab[slab_index]

    def cycle_tiles(offset):
        source = (slab_index - offset) % slab_count
        level = level_of(jnp.abs(own_frame - frame_of_slab[source]), level_count)
        return (level_tiles[level], level_allow[level])

    zero_rows = jnp.zeros((local_rows, width), jnp.float32)
    zero_pair = jnp.zeros((2, local_rows, width), jnp.float32)
    row_pair = jnp.stack([query_rows, grad_out])
    stat_pair = jnp.stack([log_norm, delta])

    def cycle_turn(offset, carry_state):
        pair, visiting, visit_stats, grad_sum, query_grad = carry_state
        pair = pass_keys(pair)
        visiting = passed_along(visiting, "slab", 1)
        visit_stats = passed_along(visit_stats, "slab", 1)
        tiles, allow = cycle_tiles(offset)
        part_q = query_side(query_rows, grad_out, log_norm, delta, pair[0], pair[1], allow)
        part_kv = key_side(
            visiting[0], visiting[1], visit_stats[0], visit_stats[1], key_rows, value_rows, allow
        )
        return (pair, visiting, visit_stats, grad_sum + part_kv, query_grad + part_q)

    loop_state = lax.fori_loop(
        1, slab_count, cycle_turn, (key_pair, row_pair, stat_pair, zero_pair, zero_rows)
    )
    grad_sum = loop_state[3]
    query_grad = loop_state[4]
    grad_query = (win_q + query_grad).astype(jnp.bfloat16)
    grad_key = (own_grads[0] + grad_sum[0]).astype(jnp.bfloat16)
    grad_value = (own_grads[1] + grad_sum[1]).astype(jnp.bfloat16)
    return (grad_query, grad_key, grad_value)


def solution(mesh):
    placed = (
        P(("slab", "space"), None),
        P(("slab", "space"), None),
        P(("slab", "space"), None),
        P(("slab", "space"), None),
        P(("slab", "space"), None),
        P(None, ("slab", "space")),
        P(),
        P(),
    )
    return jax.shard_map(
        body,
        mesh=mesh,
        in_specs=placed,
        out_specs=(
            P(("slab", "space"), None),
            P(("slab", "space"), None),
            P(("slab", "space"), None),
        ),
        check_vma=False,
    )
```

profile of v0, /device:TPU:5, one launch (start us, length us, event | category | flops | bytes accessed | tf_op | source)
XLA Modules:
  0.0 518.1 jit_solution(9312304236355362864)
XLA Ops:
  2.2 10.7 %collective-permute-start.4 = (bf16[2,256,128]{2,1,0:T(8,128)(2,1)}, bf16[2,256,128]{2,1,0:T(8,128)(2,1)S(1)}, u32[]{:S(2)}, u32[]{:S(2)}) collective-permute-start(bf16[2,256,128]{2,1,0:T(8,128)(2,1)} %pad_maximum_fusion.2), channel_id=1, source_target_pairs={{1,0},{2,1},{3,2},{4,3},{5,4},{6,5},{7,6},{8,7},{9,8},{10,9},{11,1... | collective-permute-start | bytes 393224 | tf_op jit(solution)/shard_map/ppermute | solution.py:23
  24.6 4.3 collective-permute-start.6
  30.9 484.3 %while.24 = (s32[]{:T(128)}, bf16[2,256,128]{2,1,0:T(8,128)(2,1)}, bf16[2,256,128]{2,1,0:T(8,128)(2,1)}, f32[2,1,256]{2,1,0:T(1,128)S(1)}, f32[2,256,128]{2,1,0:...) while((s32[]{:T(128)}, bf16[2,256,128]{2,1,0:T(8,128)(2,1)}, ...), condition=%wide.region_3.4_spmd.clone, body=%wide.region_1.3_spmd.clone.sunk | while | flops 118620200 | bytes 5329457 | solution.py:168
  31.0 5.3 %collective-permute-start = (bf16[2,256,128]{2,1,0:T(8,128)(2,1)}, bf16[2,256,128]{2,1,0:T(8,128)(2,1)S(1)}, u32[]{:S(2)}, u32[]{:S(2)}) collective-permute-start(bf16[2,256,128]{2,1,0:T(8,128)(2,1)} %get-tuple-element.653), channel_id=1, source_target_pairs={{496,0},{0,16},{16,32},{32,48},{48,64},{64,80},{80,96},{96,112},{1... | collective-permute-start | bytes 393224 | tf_op jit(solution)/shard_map/while/body/eval_jaxpr/ppermute | solution.py:12
  50.7 4.1 collective-permute-start.1
  69.2 4.1 collective-permute-start.2
  95.3 4.1 collective-permute-start
  101.4 4.2 collective-permute-start.2
  115.1 4.1 collective-permute-start.1
  133.0 3.9 collective-permute-start.2
  158.3 3.8 collective-permute-start
  175.8 3.9 collective-permute-start.1
  218.8 3.7 collective-permute-start
  237.3 3.8 collective-permute-start.1
  255.5 4.1 collective-permute-start.2
  269.5 3.8 collective-permute-start.1
  283.2 3.7 collective-permute-start
  318.5 3.8 collective-permute-start.2
  344.0 3.5 collective-permute-start
  379.0 3.7 collective-permute-start.2
  405.1 3.7 collective-permute-start
  423.6 3.7 collective-permute-start.1
  437.3 3.8 collective-permute-start
  443.4 3.7 collective-permute-start.2
  (648 shorter events, 314.9 us)
Async XLA Ops:
  2.2 17.4 %collective-permute-start.4 = (bf16[2,256,128]{2,1,0:T(8,128)(2,1)}, bf16[2,256,128]{2,1,0:T(8,128)(2,1)S(1)}, u32[]{:S(2)}, u32[]{:S(2)}) collective-permute-start(bf16[2,256,128]{2,1,0:T(8,128)(2,1)} %pad_maximum_fusion.2), channel_id=1, source_target_pairs={{1,0},{2,1},{3,2},{4,3},{5,4},{6,5},{7,6},{8,7},{9,8},{10,9},{11,1... | collective-permute-start | bytes 393224 | tf_op jit(solution)/shard_map/ppermute | solution.py:23
  24.6 491.8 %collective-permute-start.6 = (f32[2,256,128]{2,1,0:T(8,128)}, f32[2,256,128]{2,1,0:T(8,128)}, u32[]{:S(2)}, u32[]{:S(2)}) collective-permute-start(f32[2,256,128]{2,1,0:T(8,128)} %get-tuple-element.527), channel_id=1, source_target_pairs={{1,0},{2,1},{3,2},{4,3},{5,4},{6,5},{7,6},{8,7},{9,8},{10,9},{11,1... | collective-permute-start | bytes 786440 | tf_op jit(solution)/shard_map/ppermute | solution.py:31
  28.9 487.4 %collective-permute-start.5 = (f32[2,256,128]{2,1,0:T(8,128)}, f32[2,256,128]{2,1,0:T(8,128)}, u32[]{:S(2)}, u32[]{:S(2)}) collective-permute-start(f32[2,256,128]{2,1,0:T(8,128)} %get-tuple-element.526), channel_id=1, source_target_pairs={{0,1},{1,2},{2,3},{3,4},{4,5},{5,6},{6,7},{7,8},{8,9},{9,10},{10,1... | collective-permute-start | bytes 786440 | tf_op jit(solution)/shard_map/ppermute | solution.py:31
  31.0 16.6 %collective-permute-start = (bf16[2,256,128]{2,1,0:T(8,128)(2,1)}, bf16[2,256,128]{2,1,0:T(8,128)(2,1)S(1)}, u32[]{:S(2)}, u32[]{:S(2)}) collective-permute-start(bf16[2,256,128]{2,1,0:T(8,128)(2,1)} %get-tuple-element.653), channel_id=1, source_target_pairs={{496,0},{0,16},{16,32},{32,48},{48,64},{64,80},{80,96},{96,112},{1... | collective-permute-start | bytes 393224 | tf_op jit(solution)/shard_map/while/body/eval_jaxpr/ppermute | solution.py:12
  48.8 14.3 %collective-permute-start = (bf16[2,256,128]{2,1,0:T(8,128)(2,1)}, bf16[2,256,128]{2,1,0:T(8,128)(2,1)S(1)}, u32[]{:S(2)}, u32[]{:S(2)}) collective-permute-start(bf16[2,256,128]{2,1,0:T(8,128)(2,1)} %get-tuple-element.653), channel_id=1, source_target_pairs={{496,0},{0,16},{16,32},{32,48},{48,64},{64,80},{80,96},{96,112},{1... | collective-permute-start | bytes 393224 | tf_op jit(solution)/shard_map/while/body/eval_jaxpr/ppermute | solution.py:12
  64.3 15.4 %collective-permute-start = (bf16[2,256,128]{2,1,0:T(8,128)(2,1)}, bf16[2,256,128]{2,1,0:T(8,128)(2,1)S(1)}, u32[]{:S(2)}, u32[]{:S(2)}) collective-permute-start(bf16[2,256,128]{2,1,0:T(8,128)(2,1)} %get-tuple-element.653), channel_id=1, source_target_pairs={{496,0},{0,16},{16,32},{32,48},{48,64},{64,80},{80,96},{96,112},{1... | collective-permute-start | bytes 393224 | tf_op jit(solution)/shard_map/while/body/eval_jaxpr/ppermute | solution.py:12
  95.3 16.6 %collective-permute-start = (bf16[2,256,128]{2,1,0:T(8,128)(2,1)}, bf16[2,256,128]{2,1,0:T(8,128)(2,1)S(1)}, u32[]{:S(2)}, u32[]{:S(2)}) collective-permute-start(bf16[2,256,128]{2,1,0:T(8,128)(2,1)} %get-tuple-element.653), channel_id=1, source_target_pairs={{496,0},{0,16},{16,32},{32,48},{48,64},{64,80},{80,96},{96,112},{1... | collective-permute-start | bytes 393224 | tf_op jit(solution)/shard_map/while/body/eval_jaxpr/ppermute | solution.py:12
  113.2 14.7 %collective-permute-start = (bf16[2,256,128]{2,1,0:T(8,128)(2,1)}, bf16[2,256,128]{2,1,0:T(8,128)(2,1)S(1)}, u32[]{:S(2)}, u32[]{:S(2)}) collective-permute-start(bf16[2,256,128]{2,1,0:T(8,128)(2,1)} %get-tuple-element.653), channel_id=1, source_target_pairs={{496,0},{0,16},{16,32},{32,48},{48,64},{64,80},{80,96},{96,112},{1... | collective-permute-start | bytes 393224 | tf_op jit(solution)/shard_map/while/body/eval_jaxpr/ppermute | solution.py:12
  129.1 14.1 %collective-permute-start = (bf16[2,256,128]{2,1,0:T(8,128)(2,1)}, bf16[2,256,128]{2,1,0:T(8,128)(2,1)S(1)}, u32[]{:S(2)}, u32[]{:S(2)}) collective-permute-start(bf16[2,256,128]{2,1,0:T(8,128)(2,1)} %get-tuple-element.653), channel_id=1, source_target_pairs={{496,0},{0,16},{16,32},{32,48},{48,64},{64,80},{80,96},{96,112},{1... | collective-permute-start | bytes 393224 | tf_op jit(solution)/shard_map/while/body/eval_jaxpr/ppermute | solution.py:12
  158.3 14.3 %collective-permute-start = (bf16[2,256,128]{2,1,0:T(8,128)(2,1)}, bf16[2,256,128]{2,1,0:T(8,128)(2,1)S(1)}, u32[]{:S(2)}, u32[]{:S(2)}) collective-permute-start(bf16[2,256,128]{2,1,0:T(8,128)(2,1)} %get-tuple-element.653), channel_id=1, source_target_pairs={{496,0},{0,16},{16,32},{32,48},{48,64},{64,80},{80,96},{96,112},{1... | collective-permute-start | bytes 393224 | tf_op jit(solution)/shard_map/while/body/eval_jaxpr/ppermute | solution.py:12
  173.9 14.5 %collective-permute-start = (bf16[2,256,128]{2,1,0:T(8,128)(2,1)}, bf16[2,256,128]{2,1,0:T(8,128)(2,1)S(1)}, u32[]{:S(2)}, u32[]{:S(2)}) collective-permute-start(bf16[2,256,128]{2,1,0:T(8,128)(2,1)} %get-tuple-element.653), channel_id=1, source_target_pairs={{496,0},{0,16},{16,32},{32,48},{48,64},{64,80},{80,96},{96,112},{1... | collective-permute-start | bytes 393224 | tf_op jit(solution)/shard_map/while/body/eval_jaxpr/ppermute | solution.py:12
  218.8 15.0 %collective-permute-start = (bf16[2,256,128]{2,1,0:T(8,128)(2,1)}, bf16[2,256,128]{2,1,0:T(8,128)(2,1)S(1)}, u32[]{:S(2)}, u32[]{:S(2)}) collective-permute-start(bf16[2,256,128]{2,1,0:T(8,128)(2,1)} %get-tuple-element.653), channel_id=1, source_target_pairs={{496,0},{0,16},{16,32},{32,48},{48,64},{64,80},{80,96},{96,112},{1... | collective-permute-start | bytes 393224 | tf_op jit(solution)/shard_map/while/body/eval_jaxpr/ppermute | solution.py:12
  235.1 14.7 %collective-permute-start = (bf16[2,256,128]{2,1,0:T(8,128)(2,1)}, bf16[2,256,128]{2,1,0:T(8,128)(2,1)S(1)}, u32[]{:S(2)}, u32[]{:S(2)}) collective-permute-start(bf16[2,256,128]{2,1,0:T(8,128)(2,1)} %get-tuple-element.653), channel_id=1, source_target_pairs={{496,0},{0,16},{16,32},{32,48},{48,64},{64,80},{80,96},{96,112},{1... | collective-permute-start | bytes 393224 | tf_op jit(solution)/shard_map/while/body/eval_jaxpr/ppermute | solution.py:12
  251.0 15.0 %collective-permute-start = (bf16[2,256,128]{2,1,0:T(8,128)(2,1)}, bf16[2,256,128]{2,1,0:T(8,128)(2,1)S(1)}, u32[]{:S(2)}, u32[]{:S(2)}) collective-permute-start(bf16[2,256,128]{2,1,0:T(8,128)(2,1)} %get-tuple-element.653), channel_id=1, source_target_pairs={{496,0},{0,16},{16,32},{32,48},{48,64},{64,80},{80,96},{96,112},{1... | collective-permute-start | bytes 393224 | tf_op jit(solution)/shard_map/while/body/eval_jaxpr/ppermute | solution.py:12
  267.2 14.8 %collective-permute-start = (bf16[2,256,128]{2,1,0:T(8,128)(2,1)}, bf16[2,256,128]{2,1,0:T(8,128)(2,1)S(1)}, u32[]{:S(2)}, u32[]{:S(2)}) collective-permute-start(bf16[2,256,128]{2,1,0:T(8,128)(2,1)} %get-tuple-element.653), channel_id=1, source_target_pairs={{496,0},{0,16},{16,32},{32,48},{48,64},{64,80},{80,96},{96,112},{1... | collective-permute-start | bytes 393224 | tf_op jit(solution)/shard_map/while/body/eval_jaxpr/ppermute | solution.py:12
  283.2 14.7 %collective-permute-start = (bf16[2,256,128]{2,1,0:T(8,128)(2,1)}, bf16[2,256,128]{2,1,0:T(8,128)(2,1)S(1)}, u32[]{:S(2)}, u32[]{:S(2)}) collective-permute-start(bf16[2,256,128]{2,1,0:T(8,128)(2,1)} %get-tuple-element.653), channel_id=1, source_target_pairs={{496,0},{0,16},{16,32},{32,48},{48,64},{64,80},{80,96},{96,112},{1... | collective-permute-start | bytes 393224 | tf_op jit(solution)/shard_map/while/body/eval_jaxpr/ppermute | solution.py:12
  314.5 14.1 %collective-permute-start = (bf16[2,256,128]{2,1,0:T(8,128)(2,1)}, bf16[2,256,128]{2,1,0:T(8,128)(2,1)S(1)}, u32[]{:S(2)}, u32[]{:S(2)}) collective-permute-start(bf16[2,256,128]{2,1,0:T(8,128)(2,1)} %get-tuple-element.653), channel_id=1, source_target_pairs={{496,0},{0,16},{16,32},{32,48},{48,64},{64,80},{80,96},{96,112},{1... | collective-permute-start | bytes 393224 | tf_op jit(solution)/shard_map/while/body/eval_jaxpr/ppermute | solution.py:12
  344.0 14.5 %collective-permute-start = (bf16[2,256,128]{2,1,0:T(8,128)(2,1)}, bf16[2,256,128]{2,1,0:T(8,128)(2,1)S(1)}, u32[]{:S(2)}, u32[]{:S(2)}) collective-permute-start(bf16[2,256,128]{2,1,0:T(8,128)(2,1)} %get-tuple-element.653), channel_id=1, source_target_pairs={{496,0},{0,16},{16,32},{32,48},{48,64},{64,80},{80,96},{96,112},{1... | collective-permute-start | bytes 393224 | tf_op jit(solution)/shard_map/while/body/eval_jaxpr/ppermute | solution.py:12
  374.1 15.0 %collective-permute-start = (bf16[2,256,128]{2,1,0:T(8,128)(2,1)}, bf16[2,256,128]{2,1,0:T(8,128)(2,1)S(1)}, u32[]{:S(2)}, u32[]{:S(2)}) collective-permute-start(bf16[2,256,128]{2,1,0:T(8,128)(2,1)} %get-tuple-element.653), channel_id=1, source_target_pairs={{496,0},{0,16},{16,32},{32,48},{48,64},{64,80},{80,96},{96,112},{1... | collective-permute-start | bytes 393224 | tf_op jit(solution)/shard_map/while/body/eval_jaxpr/ppermute | solution.py:12
  405.1 15.0 %collective-permute-start = (bf16[2,256,128]{2,1,0:T(8,128)(2,1)}, bf16[2,256,128]{2,1,0:T(8,128)(2,1)S(1)}, u32[]{:S(2)}, u32[]{:S(2)}) collective-permute-start(bf16[2,256,128]{2,1,0:T(8,128)(2,1)} %get-tuple-element.653), channel_id=1, source_target_pairs={{496,0},{0,16},{16,32},{32,48},{48,64},{64,80},{80,96},{96,112},{1... | collective-permute-start | bytes 393224 | tf_op jit(solution)/shard_map/while/body/eval_jaxpr/ppermute | solution.py:12
  421.3 14.7 %collective-permute-start = (bf16[2,256,128]{2,1,0:T(8,128)(2,1)}, bf16[2,256,128]{2,1,0:T(8,128)(2,1)S(1)}, u32[]{:S(2)}, u32[]{:S(2)}) collective-permute-start(bf16[2,256,128]{2,1,0:T(8,128)(2,1)} %get-tuple-element.653), channel_id=1, source_target_pairs={{496,0},{0,16},{16,32},{32,48},{48,64},{64,80},{80,96},{96,112},{1... | collective-permute-start | bytes 393224 | tf_op jit(solution)/shard_map/while/body/eval_jaxpr/ppermute | solution.py:12
  437.3 16.2 %collective-permute-start = (bf16[2,256,128]{2,1,0:T(8,128)(2,1)}, bf16[2,256,128]{2,1,0:T(8,128)(2,1)S(1)}, u32[]{:S(2)}, u32[]{:S(2)}) collective-permute-start(bf16[2,256,128]{2,1,0:T(8,128)(2,1)} %get-tuple-element.653), channel_id=1, source_target_pairs={{496,0},{0,16},{16,32},{32,48},{48,64},{64,80},{80,96},{96,112},{1... | collective-permute-start | bytes 393224 | tf_op jit(solution)/shard_map/while/body/eval_jaxpr/ppermute | solution.py:12
  484.6 14.1 %collective-permute-start = (bf16[2,256,128]{2,1,0:T(8,128)(2,1)}, bf16[2,256,128]{2,1,0:T(8,128)(2,1)S(1)}, u32[]{:S(2)}, u32[]{:S(2)}) collective-permute-start(bf16[2,256,128]{2,1,0:T(8,128)(2,1)} %get-tuple-element.653), channel_id=1, source_target_pairs={{496,0},{0,16},{16,32},{32,48},{48,64},{64,80},{80,96},{96,112},{1... | collective-permute-start | bytes 393224 | tf_op jit(solution)/shard_map/while/body/eval_jaxpr/ppermute | solution.py:12
  499.9 14.1 %collective-permute-start = (bf16[2,256,128]{2,1,0:T(8,128)(2,1)}, bf16[2,256,128]{2,1,0:T(8,128)(2,1)S(1)}, u32[]{:S(2)}, u32[]{:S(2)}) collective-permute-start(bf16[2,256,128]{2,1,0:T(8,128)(2,1)} %get-tuple-element.653), channel_id=1, source_target_pairs={{496,0},{0,16},{16,32},{32,48},{48,64},{64,80},{80,96},{96,112},{1... | collective-permute-start | bytes 393224 | tf_op jit(solution)/shard_map/while/body/eval_jaxpr/ppermute | solution.py:12
  (80 other events, 727.5 us)
where the time goes:
time: 523 us; the launch traced here: 518 us
  starting transfers between devices  267 us (51%)
  loops' own time  105 us (20%)
  local copies, waits for them, and re-layouts  69.2 us (13%)
  matrix products  45.5 us (9%)
  other arithmetic  27.8 us (5%)
    ppermute x93, starting transfers between devices, passed_along(): return lax.ppermute(block, axis, route)  248 us
    another operation x1, loops' own time, body(): lax.fori_loop(1, slab_count, cycle_turn, (key_pair, row_pair, stat_pair,...  105 us
    while x93, local copies, waits for them, and re-layouts  40.4 us
    reduce_sum x31, other arithmetic, level_of(): return jnp.sum((distance >= powers).astype(jnp.int32))  20.5 us
    dynamic_slice x31, local copies, waits for them, and re-layouts, cycle_tiles(): level = level_of(jnp.abs(own_frame - frame_of_slab[source]), level_count)  19.1 us
    dot_general x31, matrix products, key_side(): jnp.einsum('hqk,qhd->khd', dscore.astype(jnp.bfloat16), query3, preferred...  13.5 us
    dot_general x31, matrix products, query_side(): jnp.einsum('hqk,khd->qhd', dscore.astype(jnp.bfloat16), key3, preferred_e...  11.3 us
    ppermute x1, starting transfers between devices, padded(): lax.ppermute(lax.slice_in_dim(block, 0, width, axis=dim), axis, backward)  10.7 us
  transfers between devices with their start and end apart: 97, of which 1 were waited for; matrix products, arithmetic and copies ran while one was open for 26% of the time, Pallas kernels for 0%

commit v1 on v0

v1 whole, which is shorter than its diff:
```python
import functools
import math

import jax
import jax.numpy as jnp
from jax import lax
from jax.experimental import pallas as pl
from jax.experimental.pallas import tpu as pltpu
from jax.sharding import PartitionSpec as P

MESH = pl.DeviceIdType.MESH
TILE = 128
ROWS = 256
DIM = 128
LOG2E = math.log2(math.e)
MASKED = 1e30
BF16 = jnp.bfloat16
F32 = jnp.float32

NEXT = {1: 2, 2: 3, 3: 4, 5: 6, 6: 7}
FIRST = (1, 5)


def dot_nt(a, b):
    return lax.dot_general(a, b, (((1,), (1,)), ((), ())), preferred_element_type=F32)


def dot_nn(a, b):
    return lax.dot_general(a, b, (((1,), (0,)), ((), ())), preferred_element_type=F32)


def kernel(
    slab_count,
    space_count,
    level_count,
    q_hbm,
    k_hbm,
    v_hbm,
    o_hbm,
    g_hbm,
    lse_ref,
    band,
    frames,
    dq_hbm,
    dk_hbm,
    dv_hbm,
    qg,
    stat,
    wqg,
    wstat,
    kv,
    kt,
    o_buf,
    dk_acc,
    dv_acc,
    dq_acc,
    dq_out,
    dq_in,
    wdq_out,
    wdq_in,
    kv_out,
    kv_in,
    res,
    local_sem,
    fwd_send,
    fwd_recv,
    win_send,
    win_recv,
    kv_send,
    kv_recv,
    ret_send,
    ret_recv,
    wret_send,
    wret_recv,
    kvret_send,
    kvret_recv,
):
    m = lax.axis_index("slab")
    c = lax.axis_index("space")
    group = m % 4
    base = m - group
    core = group % 2
    x_lo = group // 2
    mate = [m, base + 2 * x_lo + (1 - core), base + 2 * (1 - x_lo) + core, base + 2 * (1 - x_lo) + (1 - core)]
    up = (m + 4) % slab_count
    down = (m + slab_count - 4) % slab_count
    left = (c + space_count - 1) % space_count
    right = (c + 1) % space_count
    scale = DIM ** (-0.5)

    loads = []

    def load(src, dst):
        copy = pltpu.make_async_copy(src, dst, local_sem.at[len(loads)])
        copy.start()
        loads.append(copy)

    for t in range(2):
        rows = pl.ds(t * TILE, TILE)
        load(q_hbm.at[rows], qg.at[0, t, 0])
        load(g_hbm.at[rows], qg.at[0, t, 1])
    load(o_hbm, o_buf)
    load(k_hbm, kv.at[0, 0])
    load(v_hbm, kv.at[0, 1])

    barrier = pltpu.get_barrier_semaphore()
    for peer in (up, down, mate[1], mate[2], mate[3]):
        pl.semaphore_signal(barrier, inc=1, device_id={"slab": peer}, device_id_type=MESH)
    for peer in (left, right):
        pl.semaphore_signal(barrier, inc=1, device_id={"space": peer}, device_id_type=MESH)

    for copy in loads:
        copy.wait()

    for t in range(2):
        product = qg[0, t, 1].astype(F32) * o_buf[pl.ds(t * TILE, TILE), :].astype(F32)
        stat[0, t, 1:2, :] = jnp.sum(product.T, axis=0, keepdims=True)
        stat[0, t, 0:1, :] = lse_ref[:, t * TILE : (t + 1) * TILE] * LOG2E

    pl.semaphore_wait(barrier, 7)

    def ring_copies(src, dst, half_from):
        out = []
        for half in range(2):
            peer = up if half == 0 else down
            s_half = half_from[half]
            for part in range(2):
                out.append(
                    pltpu.make_async_remote_copy(
                        src_ref=qg.at[src, s_half, part],
                        dst_ref=qg.at[dst, half, part],
                        send_sem=fwd_send.at[dst, half, part],
                        recv_sem=fwd_recv.at[dst, half, part],
                        device_id={"slab": peer},
                        device_id_type=MESH,
                    )
                )
            out.append(
                pltpu.make_async_remote_copy(
                    src_ref=stat.at[src, s_half],
                    dst_ref=stat.at[dst, half],
                    send_sem=fwd_send.at[dst, half, 2],
                    recv_sem=fwd_recv.at[dst, half, 2],
                    device_id={"slab": peer},
                    device_id_type=MESH,
                )
            )
        return out

    hop = {
        1: ring_copies(0, 1, (0, 1)),
        2: ring_copies(1, 2, (0, 1)),
        3: ring_copies(2, 3, (0, 1)),
        4: ring_copies(3, 4, (0, 1)),
        5: ring_copies(0, 5, (1, 0)),
        6: ring_copies(5, 6, (0, 1)),
        7: ring_copies(6, 7, (0, 1)),
    }

    def start(copies):
        for copy in copies:
            copy.start()

    def arrive(step):
        onward = hop[NEXT[step]] if step in NEXT else [None] * 6
        for n in (0, 3, 1, 4, 2, 5):
            hop[step][n].wait_recv()
            if onward[n] is not None:
                onward[n].start()

    def kv_copy(src, dst, peer, n):
        return pltpu.make_async_remote_copy(
            src_ref=kv.at[src],
            dst_ref=kv.at[dst],
            send_sem=kv_send.at[n],
            recv_sem=kv_recv.at[n],
            device_id={"slab": peer},
            device_id_type=MESH,
        )

    kv1 = kv_copy(0, 1, mate[1], 0)
    kv2 = kv_copy(0, 2, mate[2], 1)
    kv3 = kv_copy(2, 3, mate[1], 2)

    def win_copies(side, peer):
        return [
            pltpu.make_async_remote_copy(
                src_ref=qg.at[0],
                dst_ref=wqg.at[side],
                send_sem=win_send.at[side, 0],
                recv_sem=win_recv.at[side, 0],
                device_id={"space": peer},
                device_id_type=MESH,
            ),
            pltpu.make_async_remote_copy(
                src_ref=stat.at[0],
                dst_ref=wstat.at[side],
                send_sem=win_send.at[side, 1],
                recv_sem=win_recv.at[side, 1],
                device_id={"space": peer},
                device_id_type=MESH,
            ),
        ]

    win = win_copies(0, right) + win_copies(1, left)
    wret = [
        pltpu.make_async_remote_copy(
            src_ref=wdq_out.at[side],
            dst_ref=wdq_in.at[side],
            send_sem=wret_send.at[side],
            recv_sem=wret_recv.at[side],
            device_id={"space": peer},
            device_id_type=MESH,
        )
        for side, peer in ((0, left), (1, right))
    ]

    def ret_copies(step):
        return [
            pltpu.make_async_remote_copy(
                src_ref=dq_out.at[step, half],
                dst_ref=dq_in.at[step, half],
                send_sem=ret_send.at[step, half],
                recv_sem=ret_recv.at[step, half],
                device_id={"slab": down if half == 0 else up},
                device_id_type=MESH,
            )
            for half in range(2)
        ]

    ret = {step: ret_copies(step) for step in range(1, 8)}

    def kvret_copy(slot, peer):
        return pltpu.make_async_remote_copy(
            src_ref=kv_out.at[slot],
            dst_ref=kv_in.at[slot],
            send_sem=kvret_send.at[slot],
            recv_sem=kvret_recv.at[slot],
            device_id={"slab": peer},
            device_id_type=MESH,
        )

    kvret = {1: kvret_copy(1, mate[1]), 2: kvret_copy(2, mate[2]), 3: kvret_copy(3, mate[1])}

    start(hop[1])
    kv2.start()
    kv1.start()
    start(win)
    start(hop[5])

    dk_acc[...] = jnp.zeros_like(dk_acc)
    dv_acc[...] = jnp.zeros_like(dv_acc)
    kt[0] = kv[0, 0].astype(F32).T.astype(BF16)

    lane = lax.broadcasted_iota(jnp.int32, (1, ROWS), 1)

    def mask_bias(level, q_tile, k_tile):
        return jnp.where(band[level, q_tile, k_tile] > 0, 0.0, MASKED).astype(F32)

    def level_between(a, b):
        distance = jnp.abs(frames[a] - frames[b])
        level = jnp.int32(0)
        for n in range(level_count - 1):
            level = level + jnp.where(distance >= 2**n, 1, 0)
        return level

    def pair(q, g, lse, delta, biases, j):
        key = kv[j, 0]
        shift = [lse + jnp.where(lane < TILE, biases[t][0], biases[t][1]) for t in range(2)]
        shifts = jnp.concatenate(
            [jnp.broadcast_to(shift[t], (TILE, ROWS)) for t in range(2)], axis=0
        )
        prob = jnp.exp2(dot_nt(key, q) * (scale * LOG2E) - shifts)
        dprob = dot_nt(kv[j, 1], g)
        dscore = (prob * (dprob - delta)).astype(BF16)
        dv_acc[j] += dot_nn(prob.astype(BF16), g)
        dk_acc[j] += dot_nn(dscore, q)
        return dot_nn(kt[j], dscore)

    def step_compute(s):
        hops = jnp.where(s <= 4, s, s - 4)
        first = jnp.where(s <= 4, 0, 1)
        source = [
            (m + slab_count - 4 * hops) % slab_count,
            (m + 4 * hops) % slab_count,
        ]
        q_tile = [2 * c + first, 2 * c + (1 - first)]
        block = [jnp.concatenate([qg[s, 0, n], qg[s, 1, n]], axis=0) for n in range(2)]
        lse = jnp.concatenate([stat[s, 0, 0:1, :], stat[s, 1, 0:1, :]], axis=1)
        delta = jnp.concatenate([stat[s, 0, 1:2, :], stat[s, 1, 1:2, :]], axis=1)
        total = jnp.zeros((DIM, ROWS), F32)
        for j in range(4):
            level = [level_between(source[half], mate[j]) for half in range(2)]
            biases = [
                [mask_bias(level[half], q_tile[half], 2 * c + t) for half in range(2)]
                for t in range(2)
            ]
            total = total + pair(block[0], block[1], lse, delta, biases, j)
        dq_acc[s] = total

    def window_compute(side):
        away = c - 1 if side == 0 else c + 1
        there = left if side == 0 else right
        inside = jnp.where((away >= 0) & (away < space_count), 1, 0)
        block = [
            jnp.concatenate([wqg[side, 0, n], wqg[side, 1, n]], axis=0) for n in range(2)
        ]
        lse = jnp.concatenate([wstat[side, 0, 0:1, :], wstat[side, 1, 0:1, :]], axis=1)
        delta = jnp.concatenate([wstat[side, 0, 1:2, :], wstat[side, 1, 1:2, :]], axis=1)
        biases = [
            [
                jnp.where(band[0, 2 * there + half, 2 * c + t] * inside > 0, 0.0, MASKED).astype(F32)
                for half in range(2)
            ]
            for t in range(2)
        ]
        part = pair(block[0], block[1], lse, delta, biases, 0)
        for half in range(2):
            wdq_out[side, half] = part[:, half * TILE : (half + 1) * TILE].astype(BF16)

    def send_back(step, prior):
        for half in range(2):
            part = dq_acc[step, :, half * TILE : (half + 1) * TILE]
            if prior is not None:
                ret[prior][half].wait_recv()
                part = part + dq_in[prior, half].astype(F32)
            dq_out[step, half] = part.astype(BF16)
            ret[step][half].start()

    arrive(1)
    kv2.wait_recv()
    kv3.start()
    for copy in win:
        copy.wait_recv()
    for side in range(2):
        window_compute(side)
        wret[side].start()
    kv1.wait_recv()
    kt[1] = kv[1, 0].astype(F32).T.astype(BF16)
    kt[2] = kv[2, 0].astype(F32).T.astype(BF16)
    kv3.wait_recv()
    kt[3] = kv[3, 0].astype(F32).T.astype(BF16)

    def turn(s, carry):
        for n in range(1, 7):
            @pl.when(s == n - 1)
            def _():
                arrive(n + 1)

        step_compute(s)

        @pl.when(s == 4)
        def _():
            send_back(4, None)

        @pl.when(s == 5)
        def _():
            send_back(3, 4)

        @pl.when(s == 6)
        def _():
            send_back(2, 3)

        return carry

    lax.fori_loop(0, 8, turn, 0)

    def pack(j, extra=None):
        dk = dk_acc[j]
        dv = dv_acc[j]
        if extra is not None:
            dk = dk + kv_in[extra, 0].astype(F32)
            dv = dv + kv_in[extra, 1].astype(F32)
        kv_out[j, 0] = dk.astype(BF16)
        kv_out[j, 1] = dv.astype(BF16)

    pack(3)
    kvret[3].start()
    send_back(7, None)
    pack(1)
    kvret[1].start()
    send_back(1, 2)
    kvret[3].wait_recv()
    pack(2, 3)
    kvret[2].start()
    send_back(6, 7)
    send_back(5, 6)

    for side in range(2):
        wret[side].wait_recv()
    total = [dq_acc[0, :, half * TILE : (half + 1) * TILE] for half in range(2)]
    for half in range(2):
        for side in range(2):
            total[half] = total[half] + wdq_in[side, half].astype(F32)
        ret[1][half].wait_recv()
        total[half] = total[half] + dq_in[1, half].astype(F32)
    for half in range(2):
        ret[5][half].wait_recv()
        total[1 - half] = total[1 - half] + dq_in[5, half].astype(F32)
    for half in range(2):
        res[0, half * TILE : (half + 1) * TILE, :] = (total[half].T * scale).astype(BF16)
    stores = [pltpu.make_async_copy(res.at[0], dq_hbm, local_sem.at[0])]
    stores[0].start()

    for slot in (1, 2):
        kvret[slot].wait_recv()
    dk = dk_acc[0] + kv_in[1, 0].astype(F32) + kv_in[2, 0].astype(F32)
    dv = dv_acc[0] + kv_in[1, 1].astype(F32) + kv_in[2, 1].astype(F32)
    res[1] = (dk * scale).astype(BF16)
    res[2] = dv.astype(BF16)
    for n, out in ((1, dk_hbm), (2, dv_hbm)):
        copy = pltpu.make_async_copy(res.at[n], out, local_sem.at[n])
        copy.start()
        stores.append(copy)

    for step in range(1, 8):
        for copy in hop[step]:
            copy.wait_send()
        for copy in ret[step]:
            copy.wait_send()
    for copy in win + wret + [kv1, kv2, kv3] + list(kvret.values()) + []:
        copy.wait_send()
    for copy in stores:
        copy.wait()


def body(slab_count, space_count, query, key, value, out_saved, grad_out, log_norm, band, frames):
    any_spec = pl.BlockSpec(memory_space=pl.ANY)
    smem = pl.BlockSpec(memory_space=pltpu.SMEM)
    vmem = pl.BlockSpec(memory_space=pltpu.VMEM)
    rows = jax.ShapeDtypeStruct((ROWS, DIM), BF16)
    dma = pltpu.SemaphoreType.DMA
    return pl.pallas_call(
        functools.partial(kernel, slab_count, space_count, band.shape[0]),
        out_shape=(rows, rows, rows),
        in_specs=[any_spec] * 5 + [vmem, smem, smem],
        out_specs=[any_spec] * 3,
        scratch_shapes=[
            pltpu.VMEM((8, 2, 2, TILE, DIM), BF16),
            pltpu.VMEM((8, 2, 2, TILE), F32),
            pltpu.VMEM((2, 2, 2, TILE, DIM), BF16),
            pltpu.VMEM((2, 2, 2, TILE), F32),
            pltpu.VMEM((4, 2, ROWS, DIM), BF16),
            pltpu.VMEM((4, DIM, ROWS), BF16),
            pltpu.VMEM((ROWS, DIM), BF16),
            pltpu.VMEM((4, ROWS, DIM), F32),
            pltpu.VMEM((4, ROWS, DIM), F32),
            pltpu.VMEM((8, DIM, ROWS), F32),
            pltpu.VMEM((8, 2, DIM, TILE), BF16),
            pltpu.VMEM((8, 2, DIM, TILE), BF16),
            pltpu.VMEM((2, 2, DIM, TILE), BF16),
            pltpu.VMEM((2, 2, DIM, TILE), BF16),
            pltpu.VMEM((4, 2, ROWS, DIM), BF16),
            pltpu.VMEM((4, 2, ROWS, DIM), BF16),
            pltpu.VMEM((3, ROWS, DIM), BF16),
            dma((8,)),
            dma((8, 2, 3)),
            dma((8, 2, 3)),
            dma((2, 2)),
            dma((2, 2)),
            dma((3,)),
            dma((3,)),
            dma((8, 2)),
            dma((8, 2)),
            dma((2,)),
            dma((2,)),
            dma((4,)),
            dma((4,)),
        ],
        compiler_params=pltpu.CompilerParams(
            collective_id=0, has_side_effects=True, vmem_limit_bytes=32 * 1024 * 1024
        ),
    )(query, key, value, out_saved, grad_out, log_norm, band, frames)


def solution(mesh):
    rows = P(("slab", "space"), None)
    return jax.shard_map(
        functools.partial(body, mesh.shape["slab"], mesh.shape["space"]),
        mesh=mesh,
        in_specs=(rows, rows, rows, rows, rows, P(None, ("slab", "space")), P(), P()),
        out_specs=(rows, rows, rows),
        check_vma=False,
    )
```

time: 523 us -> 67.8 us (0.13)
  the two profiles are of different devices: /device:TPU:5 before, /device:TPU:8 now
where the time goes in v1:
time: 67.8 us; the launch traced here: 67.4 us
  Pallas kernels  58.4 us (86%)
  local copies, waits for them, and re-layouts  8.3 us (12%)
    pallas_call x1, Pallas kernels, body(): pl.pallas_call(functools.partial(kernel, slab_count, space_count, band.sh...  58.4 us
    unnamed x19, local copies, waits for them, and re-layouts  8.3 us

profile of v1, /device:TPU:8, one launch (start us, length us, event | category | flops | bytes accessed | tf_op | source)
XLA Modules:
  0.0 67.4 jit_solution(13253679837183394731)
XLA Ops:
  0.6 0.0 copy-start
  0.6 0.9 %copy-done = s32[6,32,32]{2,1,0:T(8,128)S(1)} copy-done((s32[6,32,32]{2,1,0:T(8,128)S(1)}, s32[6,32,32]{2,1,0:T(8,128)}, u32[]{:S(2)}) %copy-start) | copy-done | bytes 24600
  1.5 0.0 copy-start.1
  1.5 0.8 %copy-done.1 = bf16[256,128]{1,0:T(8,128)(2,1)S(1)} copy-done((bf16[256,128]{1,0:T(8,128)(2,1)S(1)}, bf16[256,128]{1,0:T(8,128)(2,1)}, u32[]{:S(2)}) %copy-start.1) | copy-done | bytes 65560
  2.4 0.0 copy-start.2
  2.4 0.8 %copy-done.2 = bf16[256,128]{1,0:T(8,128)(2,1)S(1)} copy-done((bf16[256,128]{1,0:T(8,128)(2,1)S(1)}, bf16[256,128]{1,0:T(8,128)(2,1)}, u32[]{:S(2)}) %copy-start.2) | copy-done | bytes 65560
  3.2 0.0 copy-start.3
  3.2 0.8 %copy-done.3 = bf16[256,128]{1,0:T(8,128)(2,1)S(1)} copy-done((bf16[256,128]{1,0:T(8,128)(2,1)S(1)}, bf16[256,128]{1,0:T(8,128)(2,1)}, u32[]{:S(2)}) %copy-start.3) | copy-done | bytes 65560
  4.0 0.0 copy-start.4
  4.0 0.8 %copy-done.4 = bf16[256,128]{1,0:T(8,128)(2,1)S(1)} copy-done((bf16[256,128]{1,0:T(8,128)(2,1)S(1)}, bf16[256,128]{1,0:T(8,128)(2,1)}, u32[]{:S(2)}) %copy-start.4) | copy-done | bytes 65560
  4.9 0.0 copy-start.5
  4.9 0.8 %copy-done.5 = bf16[256,128]{1,0:T(8,128)(2,1)S(1)} copy-done((bf16[256,128]{1,0:T(8,128)(2,1)S(1)}, bf16[256,128]{1,0:T(8,128)(2,1)}, u32[]{:S(2)}) %copy-start.5) | copy-done | bytes 65560
  5.7 0.0 copy-start.6
  5.7 0.7 %copy-done.6 = f32[1,256]{1,0:T(1,128)S(1)} copy-done((f32[1,256]{1,0:T(1,128)S(1)}, f32[1,256]{1,0:T(1,128)}, u32[]{:S(2)}) %copy-start.6) | copy-done | bytes 1048
  6.4 0.0 copy-start.7
  6.4 0.7 copy-done.7
  7.1 58.4 %shard_map.103 = (bf16[256,128]{1,0:T(8,128)(2,1)S(1)}, bf16[256,128]{1,0:T(8,128)(2,1)S(1)}, bf16[256,128]{1,0:T(8,128)(2,1)S(1)}) custom-call(bf16[256,128]{1,0:T(8,128)(2,1)S(1)} %copy-done.1, bf16[256,128]{1,0:T(8,128)(2,1)S(1)} %copy-done.2, bf16[256,128]{1,0:T(8,128)(2,1)S(1)} %copy-done.3, bf16[256,128]{1,0:T(8,128)(2,1)S(1)} %copy-done.4, ...), custom_call_target="tpu_custom_call" | custom-call | tf_op jit(solution)/shard_map/pallas_call | solution.py:433
  65.5 0.6 copy.14
  66.1 0.6 copy.15
  66.8 0.6 copy.16
Async XLA Ops:
  0.6 0.9 %copy-start = (s32[6,32,32]{2,1,0:T(8,128)S(1)}, s32[6,32,32]{2,1,0:T(8,128)}, u32[]{:S(2)}) copy-start(s32[6,32,32]{2,1,0:T(8,128)} %band.1) | copy-start | bytes 73732
  1.5 0.8 %copy-start.1 = (bf16[256,128]{1,0:T(8,128)(2,1)S(1)}, bf16[256,128]{1,0:T(8,128)(2,1)}, u32[]{:S(2)}) copy-start(bf16[256,128]{1,0:T(8,128)(2,1)} %q_hbm.1) | copy-start | bytes 196612
  2.4 0.8 %copy-start.2 = (bf16[256,128]{1,0:T(8,128)(2,1)S(1)}, bf16[256,128]{1,0:T(8,128)(2,1)}, u32[]{:S(2)}) copy-start(bf16[256,128]{1,0:T(8,128)(2,1)} %k_hbm.1) | copy-start | bytes 196612
  3.2 0.8 %copy-start.3 = (bf16[256,128]{1,0:T(8,128)(2,1)S(1)}, bf16[256,128]{1,0:T(8,128)(2,1)}, u32[]{:S(2)}) copy-start(bf16[256,128]{1,0:T(8,128)(2,1)} %v_hbm.1) | copy-start | bytes 196612
  4.0 0.8 %copy-start.4 = (bf16[256,128]{1,0:T(8,128)(2,1)S(1)}, bf16[256,128]{1,0:T(8,128)(2,1)}, u32[]{:S(2)}) copy-start(bf16[256,128]{1,0:T(8,128)(2,1)} %o_hbm.1) | copy-start | bytes 196612
  4.9 0.8 %copy-start.5 = (bf16[256,128]{1,0:T(8,128)(2,1)S(1)}, bf16[256,128]{1,0:T(8,128)(2,1)}, u32[]{:S(2)}) copy-start(bf16[256,128]{1,0:T(8,128)(2,1)} %g_hbm.1) | copy-start | bytes 196612
  5.7 0.7 %copy-start.6 = (f32[1,256]{1,0:T(1,128)S(1)}, f32[1,256]{1,0:T(1,128)}, u32[]{:S(2)}) copy-start(f32[1,256]{1,0:T(1,128)} %lse_ref.1) | copy-start | bytes 3076
  6.4 0.7 copy-start.7

commit v2 on v1

--- a/solution.py
+++ b/solution.py
@@ -17,8 +17,8 @@
 BF16 = jnp.bfloat16
 F32 = jnp.float32
 
-NEXT = {1: 2, 2: 3, 3: 4, 5: 6, 6: 7}
-FIRST = (1, 5)
+ONWARD = {1: 3, 2: 4, 3: 5, 4: 6}
+STEPS = 8
 
 
 def dot_nt(a, b):
@@ -103,8 +103,12 @@
     load(k_hbm, kv.at[0, 0])
     load(v_hbm, kv.at[0, 1])
 
+    def ring(hops):
+        return (m + 4 * hops + slab_count) % slab_count
+
     barrier = pltpu.get_barrier_semaphore()
-    for peer in (up, down, mate[1], mate[2], mate[3]):
+    peers = [ring(hops) for hops in (-3, -2, -1, 1, 2, 3, 4)] + mate[1:]
+    for peer in peers:
         pl.semaphore_signal(barrier, inc=1, device_id={"slab": peer}, device_id_type=MESH)
     for peer in (left, right):
         pl.semaphore_signal(barrier, inc=1, device_id={"space": peer}, device_id_type=MESH)
@@ -117,56 +121,40 @@
         stat[0, t, 1:2, :] = jnp.sum(product.T, axis=0, keepdims=True)
         stat[0, t, 0:1, :] = lse_ref[:, t * TILE : (t + 1) * TILE] * LOG2E
 
-    pl.semaphore_wait(barrier, 7)
-
-    def ring_copies(src, dst, half_from):
-        out = []
-        for half in range(2):
-            peer = up if half == 0 else down
-            s_half = half_from[half]
-            for part in range(2):
-                out.append(
-                    pltpu.make_async_remote_copy(
-                        src_ref=qg.at[src, s_half, part],
-                        dst_ref=qg.at[dst, half, part],
-                        send_sem=fwd_send.at[dst, half, part],
-                        recv_sem=fwd_recv.at[dst, half, part],
-                        device_id={"slab": peer},
-                        device_id_type=MESH,
-                    )
-                )
-            out.append(
-                pltpu.make_async_remote_copy(
-                    src_ref=stat.at[src, s_half],
-                    dst_ref=stat.at[dst, half],
-                    send_sem=fwd_send.at[dst, half, 2],
-                    recv_sem=fwd_recv.at[dst, half, 2],
+    pl.semaphore_wait(barrier, len(peers) + 2)
+
+    def frame_copies(src, dst, peer, tiles=(0, 1)):
+        out = {}
+        for tile in tiles:
+            for part in range(3):
+                big = part < 2
+                out[tile, part] = pltpu.make_async_remote_copy(
+                    src_ref=qg.at[src, tile, part] if big else stat.at[src, tile],
+                    dst_ref=qg.at[dst, tile, part] if big else stat.at[dst, tile],
+                    send_sem=fwd_send.at[dst, tile, part],
+                    recv_sem=fwd_recv.at[dst, tile, part],
                     device_id={"slab": peer},
                     device_id_type=MESH,
                 )
-            )
         return out
 
-    hop = {
-        1: ring_copies(0, 1, (0, 1)),
-        2: ring_copies(1, 2, (0, 1)),
-        3: ring_copies(2, 3, (0, 1)),
-        4: ring_copies(3, 4, (0, 1)),
-        5: ring_copies(0, 5, (1, 0)),
-        6: ring_copies(5, 6, (0, 1)),
-        7: ring_copies(6, 7, (0, 1)),
-    }
+    hop = {}
+    for s in range(1, 7):
+        hop[s] = frame_copies(max(s - 2, 0), s, up if s % 2 else down)
+    far = {0: frame_copies(3, 7, ring(2), (0,)), 1: frame_copies(4, 7, ring(-2), (1,))}
+    hop[7] = {**far[0], **far[1]}
 
     def start(copies):
-        for copy in copies:
+        for copy in copies.values():
             copy.start()
 
     def arrive(step):
-        onward = hop[NEXT[step]] if step in NEXT else [None] * 6
-        for n in (0, 3, 1, 4, 2, 5):
-            hop[step][n].wait_recv()
-            if onward[n] is not None:
-                onward[n].start()
+        for key, copy in hop[step].items():
+            copy.wait_recv()
+            if step in (3, 4) and key[0] == step - 3:
+                hop[7][key].start()
+            if step in ONWARD:
+                hop[ONWARD[step]][key].start()
 
     def kv_copy(src, dst, peer, n):
         return pltpu.make_async_remote_copy(
@@ -215,20 +203,18 @@
         for side, peer in ((0, left), (1, right))
     ]
 
-    def ret_copies(step):
-        return [
-            pltpu.make_async_remote_copy(
-                src_ref=dq_out.at[step, half],
-                dst_ref=dq_in.at[step, half],
-                send_sem=ret_send.at[step, half],
-                recv_sem=ret_recv.at[step, half],
-                device_id={"slab": down if half == 0 else up},
-                device_id_type=MESH,
-            )
-            for half in range(2)
-        ]
-
-    ret = {step: ret_copies(step) for step in range(1, 8)}
+    def source(step):
+        return ring(jnp.where(step % 2 == 1, -1, 1) * ((step + 1) // 2))
+
+    def ret(step):
+        return pltpu.make_async_remote_copy(
+            src_ref=dq_out.at[step],
+            dst_ref=dq_in.at[step],
+            send_sem=ret_send.at[step],
+            recv_sem=ret_recv.at[step],
+            device_id={"slab": source(step)},
+            device_id_type=MESH,
+        )
 
     def kvret_copy(slot, peer):
         return pltpu.make_async_remote_copy(
@@ -243,10 +229,11 @@
     kvret = {1: kvret_copy(1, mate[1]), 2: kvret_copy(2, mate[2]), 3: kvret_copy(3, mate[1])}
 
     start(hop[1])
+    start(hop[2])
     kv2.start()
     kv1.start()
-    start(win)
-    start(hop[5])
+    for copy in win:
+        copy.start()
 
     dk_acc[...] = jnp.zeros_like(dk_acc)
     dv_acc[...] = jnp.zeros_like(dv_acc)
@@ -277,26 +264,18 @@
         dk_acc[j] += dot_nn(dscore, q)
         return dot_nn(kt[j], dscore)
 
-    def step_compute(s):
-        hops = jnp.where(s <= 4, s, s - 4)
-        first = jnp.where(s <= 4, 0, 1)
-        source = [
-            (m + slab_count - 4 * hops) % slab_count,
-            (m + 4 * hops) % slab_count,
+    def frame(s):
+        block = [jnp.concatenate([qg[s, 0, n], qg[s, 1, n]], axis=0) for n in range(2)]
+        row = [
+            jnp.concatenate([stat[s, 0, n : n + 1, :], stat[s, 1, n : n + 1, :]], axis=1)
+            for n in range(2)
         ]
-        q_tile = [2 * c + first, 2 * c + (1 - first)]
-        block = [jnp.concatenate([qg[s, 0, n], qg[s, 1, n]], axis=0) for n in range(2)]
-        lse = jnp.concatenate([stat[s, 0, 0:1, :], stat[s, 1, 0:1, :]], axis=1)
-        delta = jnp.concatenate([stat[s, 0, 1:2, :], stat[s, 1, 1:2, :]], axis=1)
-        total = jnp.zeros((DIM, ROWS), F32)
-        for j in range(4):
-            level = [level_between(source[half], mate[j]) for half in range(2)]
-            biases = [
-                [mask_bias(level[half], q_tile[half], 2 * c + t) for half in range(2)]
-                for t in range(2)
-            ]
-            total = total + pair(block[0], block[1], lse, delta, biases, j)
-        dq_acc[s] = total
+        return block + row
+
+    def visit(s, j):
+        level = level_between(source(s) if not isinstance(s, int) else m, mate[j])
+        biases = [[mask_bias(level, 2 * c + h, 2 * c + t) for h in range(2)] for t in range(2)]
+        return pair(*frame(s), biases, j)
 
     def window_compute(side):
         away = c - 1 if side == 0 else c + 1
@@ -315,55 +294,44 @@
             for t in range(2)
         ]
         part = pair(block[0], block[1], lse, delta, biases, 0)
-        for half in range(2):
-            wdq_out[side, half] = part[:, half * TILE : (half + 1) * TILE].astype(BF16)
-
-    def send_back(step, prior):
-        for half in range(2):
-            part = dq_acc[step, :, half * TILE : (half + 1) * TILE]
-            if prior is not None:
-                ret[prior][half].wait_recv()
-                part = part + dq_in[prior, half].astype(F32)
-            dq_out[step, half] = part.astype(BF16)
-            ret[step][half].start()
-
+        wdq_out[side] = part.astype(BF16)
+
+    def key_t(j):
+        kt[j] = kv[j, 0].astype(F32).T.astype(BF16)
+
+    dq_acc[...] = visit(0, 0)
+    kv1.wait_recv()
+    key_t(1)
+    dq_acc[...] += visit(0, 1)
     arrive(1)
+    arrive(2)
     kv2.wait_recv()
     kv3.start()
+    key_t(2)
+    dq_acc[...] += visit(0, 2)
     for copy in win:
         copy.wait_recv()
     for side in range(2):
         window_compute(side)
         wret[side].start()
-    kv1.wait_recv()
-    kt[1] = kv[1, 0].astype(F32).T.astype(BF16)
-    kt[2] = kv[2, 0].astype(F32).T.astype(BF16)
     kv3.wait_recv()
-    kt[3] = kv[3, 0].astype(F32).T.astype(BF16)
+    key_t(3)
+    dq_acc[...] += visit(0, 3)
 
     def turn(s, carry):
-        for n in range(1, 7):
-            @pl.when(s == n - 1)
+        for n in range(1, 6):
+            @pl.when(s == n)
             def _():
-                arrive(n + 1)
-
-        step_compute(s)
-
-        @pl.when(s == 4)
-        def _():
-            send_back(4, None)
-
-        @pl.when(s == 5)
-        def _():
-            send_back(3, 4)
-
-        @pl.when(s == 6)
-        def _():
-            send_back(2, 3)
-
+                arrive(n + 2)
+
+        total = visit(s, 0)
+        for j in range(1, 4):
+            total = total + visit(s, j)
+        dq_out[s] = total.astype(BF16)
+        ret(s).start()
         return carry
 
-    lax.fori_loop(0, 8, turn, 0)
+    lax.fori_loop(1, STEPS, turn, 0)
 
     def pack(j, extra=None):
         dk = dk_acc[j]
@@ -376,29 +344,20 @@
 
     pack(3)
     kvret[3].start()
-    send_back(7, None)
     pack(1)
     kvret[1].start()
-    send_back(1, 2)
     kvret[3].wait_recv()
     pack(2, 3)
     kvret[2].start()
-    send_back(6, 7)
-    send_back(5, 6)
-
+
+    total = dq_acc[...]
     for side in range(2):
         wret[side].wait_recv()
-    total = [dq_acc[0, :, half * TILE : (half + 1) * TILE] for half in range(2)]
-    for half in range(2):
-        for side in range(2):
-            total[half] = total[half] + wdq_in[side, half].astype(F32)
-        ret[1][half].wait_recv()
-        total[half] = total[half] + dq_in[1, half].astype(F32)
-    for half in range(2):
-        ret[5][half].wait_recv()
-        total[1 - half] = total[1 - half] + dq_in[5, half].astype(F32)
-    for half in range(2):
-        res[0, half * TILE : (half + 1) * TILE, :] = (total[half].T * scale).astype(BF16)
+        total = total + wdq_in[side].astype(F32)
+    for step in range(1, STEPS):
+        ret(jnp.int32(step)).wait_recv()
+        total = total + dq_in[step].astype(F32)
+    res[0] = (total.T * scale).astype(BF16)
     stores = [pltpu.make_async_copy(res.at[0], dq_hbm, local_sem.at[0])]
     stores[0].start()
 
@@ -413,12 +372,11 @@
         copy.start()
         stores.append(copy)
 
-    for step in range(1, 8):
-        for copy in hop[step]:
+    for step in range(1, STEPS):
+        for copy in hop[step].values():
             copy.wait_send()
-        for copy in ret[step]:
-            copy.wait_send()
-    for copy in win + wret + [kv1, kv2, kv3] + list(kvret.values()) + []:
+        ret(jnp.int32(step)).wait_send()
+    for copy in win + wret + [kv1, kv2, kv3] + list(kvret.values()):
         copy.wait_send()
     for copy in stores:
         copy.wait()
@@ -445,11 +403,11 @@
             pltpu.VMEM((ROWS, DIM), BF16),
             pltpu.VMEM((4, ROWS, DIM), F32),
             pltpu.VMEM((4, ROWS, DIM), F32),
-            pltpu.VMEM((8, DIM, ROWS), F32),
-            pltpu.VMEM((8, 2, DIM, TILE), BF16),
-            pltpu.VMEM((8, 2, DIM, TILE), BF16),
-            pltpu.VMEM((2, 2, DIM, TILE), BF16),
-            pltpu.VMEM((2, 2, DIM, TILE), BF16),
+            pltpu.VMEM((DIM, ROWS), F32),
+            pltpu.VMEM((8, DIM, ROWS), BF16),
+            pltpu.VMEM((8, DIM, ROWS), BF16),
+            pltpu.VMEM((2, DIM, ROWS), BF16),
+            pltpu.VMEM((2, DIM, ROWS), BF16),
             pltpu.VMEM((4, 2, ROWS, DIM), BF16),
             pltpu.VMEM((4, 2, ROWS, DIM), BF16),
             pltpu.VMEM((3, ROWS, DIM), BF16),
@@ -460,15 +418,15 @@
             dma((2, 2)),
             dma((3,)),
             dma((3,)),
-            dma((8, 2)),
-            dma((8, 2)),
+            dma((8,)),
+            dma((8,)),
             dma((2,)),
             dma((2,)),
             dma((4,)),
             dma((4,)),
         ],
         compiler_params=pltpu.CompilerParams(
-            collective_id=0, has_side_effects=True, vmem_limit_bytes=32 * 1024 * 1024
+            collective_id=0, has_side_effects=True, vmem_limit_bytes=63 * 1024 * 1024
         ),
     )(query, key, value, out_saved, grad_out, log_norm, band, frames)
 

time: 67.8 us -> 54.9 us (0.81)
  the two profiles are of different devices: /device:TPU:8 before, /device:TPU:2 now
where the time goes in v2:
time: 54.9 us; the launch traced here: 54.6 us
  Pallas kernels  50.9 us (93%)
  local copies, waits for them, and re-layouts  3 us (5%)
  between operations  0.65 us (1%)
    pallas_call x1, Pallas kernels, body(): pl.pallas_call(functools.partial(kernel, slab_count, space_count, band.sh...  50.9 us
    unnamed x7, local copies, waits for them, and re-layouts  3 us

profile of v2, /device:TPU:2, one launch (start us, length us, event | category | flops | bytes accessed | tf_op | source)
XLA Modules:
  0.0 54.6 jit_solution(13016166567688312985)
XLA Ops:
  0.6 50.9 %shard_map.103 = (bf16[256,128]{1,0:T(8,128)(2,1)}, bf16[256,128]{1,0:T(8,128)(2,1)}, bf16[256,128]{1,0:T(8,128)(2,1)}) custom-call(bf16[256,128]{1,0:T(8,128)(2,1)} %q_hbm.1, bf16[256,128]{1,0:T(8,128)(2,1)} %k_hbm.1, bf16[256,128]{1,0:T(8,128)(2,1)} %v_hbm.1, bf16[256,128]{1,0:T(8,128)(2,1)} %o_hbm.1, bf16[256,128]{1,0:T(8,128)(2,1)} %g_hbm.1, ...), custom_call_target="tpu_custom_call" | custom-call | tf_op jit(solution)/shard_map/pallas_call | solution.py:391
  51.6 0.0 copy-start.1
  51.6 1.5 %copy.14 = bf16[256,128]{1,0:T(8,128)(2,1)} copy(bf16[256,128]{1,0:T(8,128)(2,1)} %get-tuple-element.6) | data formatting | bytes 131072
  53.1 0.0 copy-done.1
  53.1 0.0 copy-start
  53.1 0.6 %copy.15 = bf16[256,128]{1,0:T(8,128)(2,1)} copy(bf16[256,128]{1,0:T(8,128)(2,1)S(1)} %copy-done.1) | data formatting | bytes 131072
  53.7 0.2 copy-done
  54.0 0.6 %copy.16 = bf16[256,128]{1,0:T(8,128)(2,1)} copy(bf16[256,128]{1,0:T(8,128)(2,1)S(1)} %copy-done) | data formatting | bytes 131072
Async XLA Ops:
  51.6 1.5 %copy-start.1 = (bf16[256,128]{1,0:T(8,128)(2,1)S(1)}, bf16[256,128]{1,0:T(8,128)(2,1)}, u32[]{:S(2)}) copy-start(bf16[256,128]{1,0:T(8,128)(2,1)} %get-tuple-element.7) | copy-start | bytes 196612
  53.1 0.9 %copy-start = (bf16[256,128]{1,0:T(8,128)(2,1)S(1)}, bf16[256,128]{1,0:T(8,128)(2,1)}, u32[]{:S(2)}) copy-start(bf16[256,128]{1,0:T(8,128)(2,1)} %get-tuple-element.8) | copy-start | bytes 196612

commit v3 on v2

v3 whole, which is shorter than its diff:
```python
import functools
import math

import jax
import jax.numpy as jnp
from jax import lax
from jax.experimental import pallas as pl
from jax.experimental.pallas import tpu as pltpu
from jax.sharding import PartitionSpec as P

MESH = pl.DeviceIdType.MESH
TILE = 128
ROWS = 256
DIM = 128
LOG2E = math.log2(math.e)
MASKED = 1e30
BF16 = jnp.bfloat16
F32 = jnp.float32

ONWARD = {1: 3, 2: 4, 3: 5, 4: 6}
STEPS = 8


def dot_nt(a, b):
    return lax.dot_general(a, b, (((1,), (1,)), ((), ())), preferred_element_type=F32)


def dot_nn(a, b):
    return lax.dot_general(a, b, (((1,), (0,)), ((), ())), preferred_element_type=F32)


def kernel(
    slab_count,
    space_count,
    level_count,
    q_hbm,
    k_hbm,
    v_hbm,
    o_hbm,
    g_hbm,
    lse_ref,
    band,
    frames,
    dq_hbm,
    dk_hbm,
    dv_hbm,
    qg,
    stat,
    wqg,
    wstat,
    kv,
    kt,
    o_buf,
    dk_acc,
    dv_acc,
    dq_acc,
    dq_out,
    dq_in,
    wdq_out,
    wdq_in,
    kv_out,
    kv_in,
    res,
    local_sem,
    fwd_send,
    fwd_recv,
    win_send,
    win_recv,
    kv_send,
    kv_recv,
    ret_send,
    ret_recv,
    wret_send,
    wret_recv,
    kvret_send,
    kvret_recv,
):
    m = lax.axis_index("slab")
    c = lax.axis_index("space")
    group = m % 4
    base = m - group
    core = group % 2
    x_lo = group // 2
    mate = [
        m,
        base + 2 * x_lo + (1 - core),
        base + 2 * (1 - x_lo) + core,
        base + 2 * (1 - x_lo) + (1 - core),
    ]
    scale = DIM ** (-0.5)
    has = [c > 0, c < space_count - 1]
    beside = [jnp.maximum(c - 1, 0), jnp.minimum(c + 1, space_count - 1)]
    odd = c % 2 == 1

    def ring(hops):
        return (m + 4 * hops + slab_count) % slab_count

    up, down = ring(1), ring(-1)

    barrier = pltpu.get_barrier_semaphore()
    for peer in (up, down, mate[2], mate[1]):
        pl.semaphore_signal(barrier, inc=1, device_id={"slab": peer}, device_id_type=MESH)
    for side in range(2):
        @pl.when(has[side] & jnp.logical_not(odd))
        def _():
            pl.semaphore_signal(
                barrier, inc=1, device_id={"space": beside[side]}, device_id_type=MESH
            )

    loads = [
        pltpu.make_async_copy(src, dst, local_sem.at[n])
        for n, (src, dst) in enumerate(
            (
                (g_hbm, qg.at[0, 1]),
                (o_hbm, o_buf),
                (k_hbm, kv.at[0, 0]),
                (q_hbm, qg.at[0, 0]),
                (v_hbm, kv.at[0, 1]),
            )
        )
    ]
    for copy in loads:
        copy.start()

    def remote(src, dst, sems, index, peer):
        return pltpu.make_async_remote_copy(
            src_ref=src,
            dst_ref=dst,
            send_sem=sems[0].at[index],
            recv_sem=sems[1].at[index],
            device_id=peer,
            device_id_type=MESH,
        )

    fwd, kvs, wins = (fwd_send, fwd_recv), (kv_send, kv_recv), (win_send, win_recv)
    own = (q_hbm, g_hbm)

    def frame_copies(src, dst, peer, tiles=(0, 1)):
        out = {}
        for tile in tiles:
            rows = pl.ds(tile * TILE, TILE)
            for part in range(2):
                source_ref = own[part].at[rows] if src == 0 else qg.at[src, part, rows]
                out[tile, part] = remote(
                    source_ref, qg.at[dst, part, rows], fwd, (dst, tile, part), {"slab": peer}
                )
            out[tile, 2] = remote(
                stat.at[src, tile], stat.at[dst, tile], fwd, (dst, tile, 2), {"slab": peer}
            )
        return out

    hop = {}
    for s in range(1, 7):
        hop[s] = frame_copies(max(s - 2, 0), s, up if s % 2 else down)
    far = {0: frame_copies(3, 7, ring(2), (0,)), 1: frame_copies(4, 7, ring(-2), (1,))}
    hop[7] = {**far[0], **far[1]}

    def arrive(step):
        for key, copy in hop[step].items():
            copy.wait_recv()
            if step in ONWARD:
                hop[ONWARD[step]][key].start()
        if step == 4:
            for copy in hop[7].values():
                copy.start()

    kv1 = [remote(h, kv.at[1, n], kvs, n, {"slab": mate[1]}) for n, h in enumerate((k_hbm, v_hbm))]
    kv2 = [
        remote(h, kv.at[2, n], kvs, 2 + n, {"slab": mate[2]}) for n, h in enumerate((k_hbm, v_hbm))
    ]
    kv3 = remote(kv.at[2], kv.at[3], kvs, 4, {"slab": mate[1]})

    win = [
        [
            remote(q_hbm, wqg.at[side, 0], wins, (side, 0), {"space": beside[1 - side]}),
            remote(g_hbm, wqg.at[side, 1], wins, (side, 1), {"space": beside[1 - side]}),
            remote(stat.at[0], wstat.at[side], wins, (side, 2), {"space": beside[1 - side]}),
        ]
        for side in range(2)
    ]
    wret = [
        remote(
            wdq_out.at[side], wdq_in.at[side], (wret_send, wret_recv), side, {"space": beside[side]}
        )
        for side in range(2)
    ]

    def source(step):
        return ring(jnp.where(step % 2 == 1, -1, 1) * ((step + 1) // 2))

    def ret(step):
        return remote(
            dq_out.at[step], dq_in.at[step], (ret_send, ret_recv), step, {"slab": source(step)}
        )

    kvret = {
        slot: remote(
            kv_out.at[slot], kv_in.at[slot], (kvret_send, kvret_recv), slot, {"slab": mate[peer]}
        )
        for slot, peer in ((1, 1), (2, 2), (3, 1))
    }

    pl.semaphore_wait(
        barrier, 4 + jnp.where(odd, has[0].astype(jnp.int32) + has[1].astype(jnp.int32), 0)
    )

    for key in ((0, 0), (0, 1), (1, 0), (1, 1)):
        hop[1][key].start()
        hop[2][key].start()
    for copy in kv2 + kv1:
        copy.start()

    for copy in loads[:2]:
        copy.wait()
    for t in range(2):
        rows = pl.ds(t * TILE, TILE)
        product = qg[0, 1, rows, :].astype(F32) * o_buf[rows, :].astype(F32)
        stat[0, t, 1:2, :] = jnp.sum(product.T, axis=0, keepdims=True)
        stat[0, t, 0:1, :] = lse_ref[:, t * TILE : (t + 1) * TILE] * LOG2E
    for tile in range(2):
        hop[1][tile, 2].start()
        hop[2][tile, 2].start()

    def win_start(side):
        for copy in win[side]:
            copy.start()

    for side in range(2):
        @pl.when(odd & has[1 - side])
        def _():
            win_start(side)

    for copy in loads[2:]:
        copy.wait()

    lane = lax.broadcasted_iota(jnp.int32, (1, ROWS), 1)

    def mask_bias(level, q_tile, k_tile):
        return jnp.where(band[level, q_tile, k_tile] > 0, 0.0, MASKED).astype(F32)

    def level_between(a, b):
        distance = jnp.abs(frames[a] - frames[b])
        level = jnp.int32(0)
        for n in range(level_count - 1):
            level = level + jnp.where(distance >= 2**n, 1, 0)
        return level

    def key_t(j):
        kt[j] = kv[j, 0].astype(F32).T.astype(BF16)

    def pair(q, g, lse, delta, biases, j, fresh=False):
        key = kv[j, 0]
        shift = [lse + jnp.where(lane < TILE, biases[t][0], biases[t][1]) for t in range(2)]
        shifts = jnp.concatenate(
            [jnp.broadcast_to(shift[t], (TILE, ROWS)) for t in range(2)], axis=0
        )
        prob = jnp.exp2(dot_nt(key, q) * (scale * LOG2E) - shifts)
        dprob = dot_nt(kv[j, 1], g)
        dscore = (prob * (dprob - delta)).astype(BF16)
        dv = dot_nn(prob.astype(BF16), g)
        dk = dot_nn(dscore, q)
        dv_acc[j] = dv if fresh else dv_acc[j] + dv
        dk_acc[j] = dk if fresh else dk_acc[j] + dk
        return dot_nn(kt[j], dscore)

    def frame(block, rows, s):
        return [block[s, 0], block[s, 1]] + [
            jnp.concatenate([rows[s, 0, n : n + 1, :], rows[s, 1, n : n + 1, :]], axis=1)
            for n in range(2)
        ]

    def visit(s, j, fresh=False):
        level = level_between(source(s), mate[j]) if not fresh else level_between(m, mate[j])
        biases = [[mask_bias(level, 2 * c + h, 2 * c + t) for h in range(2)] for t in range(2)]
        return pair(*frame(qg, stat, s), biases, j, fresh)

    key_t(0)
    dq_acc[...] = visit(0, 0, True)
    for copy in kv1:
        copy.wait_recv()
    key_t(1)
    dq_acc[...] += visit(0, 1, True)
    arrive(1)
    arrive(2)
    for copy in kv2:
        copy.wait_recv()
    kv3.start()
    key_t(2)
    dq_acc[...] += visit(0, 2, True)
    kv3.wait_recv()
    key_t(3)
    dq_acc[...] += visit(0, 3, True)

    def turn(s, carry):
        for n in range(1, 6):
            @pl.when(s == n)
            def _():
                arrive(n + 2)

        @pl.when(s == 4)
        def _():
            for side in range(2):
                @pl.when(has[side] & jnp.logical_not(odd))
                def _():
                    for copy in win[side]:
                        copy.wait_recv()
                    win_start(1 - side)

        total = visit(s, 0)
        for j in range(1, 4):
            total = total + visit(s, j)
        dq_out[s] = total.astype(BF16)
        ret(s).start()
        return carry

    lax.fori_loop(1, STEPS - 1, turn, 0)

    def pack(j, extra=None):
        dk = dk_acc[j]
        dv = dv_acc[j]
        if extra is not None:
            dk = dk + kv_in[extra, 0].astype(F32)
            dv = dv + kv_in[extra, 1].astype(F32)
        kv_out[j, 0] = dk.astype(BF16)
        kv_out[j, 1] = dv.astype(BF16)

    last = jnp.int32(STEPS - 1)
    total = visit(last, 3)
    pack(3)
    kvret[3].start()
    for j in (2, 1, 0):
        total = total + visit(last, j)
    dq_out[last] = total.astype(BF16)
    ret(last).start()
    pack(1)
    kvret[1].start()
    kvret[3].wait_recv()
    pack(2, 3)
    kvret[2].start()

    for side in range(2):
        @pl.when(has[side])
        def _():
            @pl.when(odd)
            def _():
                for copy in win[side]:
                    copy.wait_recv()
            biases = [
                [mask_bias(0, 2 * beside[side] + h, 2 * c + t) for h in range(2)] for t in range(2)
            ]
            wdq_out[side] = pair(*frame(wqg, wstat, side), biases, 0).astype(BF16)
            wret[side].start()

    for side in range(2):
        @pl.when(has[1 - side])
        def _():
            wret[side].wait_recv()
            dq_acc[...] += wdq_in[side].astype(F32)
    total = dq_acc[...]
    for step in range(1, STEPS):
        ret(jnp.int32(step)).wait_recv()
        total = total + dq_in[step].astype(F32)
    res[0] = (total.T * scale).astype(BF16)
    stores = [pltpu.make_async_copy(res.at[0], dq_hbm, local_sem.at[0])]
    stores[0].start()

    for slot in (1, 2):
        kvret[slot].wait_recv()
    dk = dk_acc[0] + kv_in[1, 0].astype(F32) + kv_in[2, 0].astype(F32)
    dv = dv_acc[0] + kv_in[1, 1].astype(F32) + kv_in[2, 1].astype(F32)
    res[1] = (dk * scale).astype(BF16)
    res[2] = dv.astype(BF16)
    for n, out in ((1, dk_hbm), (2, dv_hbm)):
        copy = pltpu.make_async_copy(res.at[n], out, local_sem.at[n])
        copy.start()
        stores.append(copy)

    for step in range(1, STEPS):
        for copy in hop[step].values():
            copy.wait_send()
        ret(jnp.int32(step)).wait_send()
    for copy in kv1 + kv2 + [kv3] + list(kvret.values()):
        copy.wait_send()
    for side in range(2):
        @pl.when(has[side])
        def _():
            for copy in win[1 - side]:
                copy.wait_send()
            wret[side].wait_send()
    for copy in stores:
        copy.wait()


def body(slab_count, space_count, query, key, value, out_saved, grad_out, log_norm, band, frames):
    any_spec = pl.BlockSpec(memory_space=pl.ANY)
    smem = pl.BlockSpec(memory_space=pltpu.SMEM)
    vmem = pl.BlockSpec(memory_space=pltpu.VMEM)
    rows = jax.ShapeDtypeStruct((ROWS, DIM), BF16)
    dma = pltpu.SemaphoreType.DMA
    return pl.pallas_call(
        functools.partial(kernel, slab_count, space_count, band.shape[0]),
        out_shape=(rows, rows, rows),
        in_specs=[any_spec] * 5 + [vmem, smem, smem],
        out_specs=[any_spec] * 3,
        scratch_shapes=[
            pltpu.VMEM((8, 2, ROWS, DIM), BF16),
            pltpu.VMEM((8, 2, 2, TILE), F32),
            pltpu.VMEM((2, 2, ROWS, DIM), BF16),
            pltpu.VMEM((2, 2, 2, TILE), F32),
            pltpu.VMEM((4, 2, ROWS, DIM), BF16),
            pltpu.VMEM((4, DIM, ROWS), BF16),
            pltpu.VMEM((ROWS, DIM), BF16),
            pltpu.VMEM((4, ROWS, DIM), F32),
            pltpu.VMEM((4, ROWS, DIM), F32),
            pltpu.VMEM((DIM, ROWS), F32),
            pltpu.VMEM((8, DIM, ROWS), BF16),
            pltpu.VMEM((8, DIM, ROWS), BF16),
            pltpu.VMEM((2, DIM, ROWS), BF16),
            pltpu.VMEM((2, DIM, ROWS), BF16),
            pltpu.VMEM((4, 2, ROWS, DIM), BF16),
            pltpu.VMEM((4, 2, ROWS, DIM), BF16),
            pltpu.VMEM((3, ROWS, DIM), BF16),
            dma((8,)),
            dma((8, 2, 3)),
            dma((8, 2, 3)),
            dma((2, 3)),
            dma((2, 3)),
            dma((5,)),
            dma((5,)),
            dma((8,)),
            dma((8,)),
            dma((2,)),
            dma((2,)),
            dma((4,)),
            dma((4,)),
        ],
        compiler_params=pltpu.CompilerParams(
            collective_id=0, has_side_effects=True, vmem_limit_bytes=63 * 1024 * 1024
        ),
    )(query, key, value, out_saved, grad_out, log_norm, band, frames)


def solution(mesh):
    rows = P(("slab", "space"), None)
    return jax.shard_map(
        functools.partial(body, mesh.shape["slab"], mesh.shape["space"]),
        mesh=mesh,
        in_specs=(rows, rows, rows, rows, rows, P(None, ("slab", "space")), P(), P()),
        out_specs=(rows, rows, rows),
        check_vma=False,
    )
```

time: 54.9 us -> 51.6 us (0.940)
  the two profiles are of different devices: /device:TPU:2 before, /device:TPU:23 now
where the time goes in v3:
time: 51.6 us; the launch traced here: 51.3 us
  Pallas kernels  47.6 us (92%)
  local copies, waits for them, and re-layouts  3 us (6%)
  between operations  0.65 us (1%)
    pallas_call x1, Pallas kernels, body(): pl.pallas_call(functools.partial(kernel, slab_count, space_count, band.sh...  47.6 us
    unnamed x7, local copies, waits for them, and re-layouts  3 us

profile of v3, /device:TPU:23, one launch (start us, length us, event | category | flops | bytes accessed | tf_op | source)
XLA Modules:
  0.0 51.3 jit_solution(12337480809235778399)
XLA Ops:
  0.6 47.6 %shard_map.103 = (bf16[256,128]{1,0:T(8,128)(2,1)}, bf16[256,128]{1,0:T(8,128)(2,1)}, bf16[256,128]{1,0:T(8,128)(2,1)}) custom-call(bf16[256,128]{1,0:T(8,128)(2,1)} %q_hbm.1, bf16[256,128]{1,0:T(8,128)(2,1)} %k_hbm.1, bf16[256,128]{1,0:T(8,128)(2,1)} %v_hbm.1, bf16[256,128]{1,0:T(8,128)(2,1)} %o_hbm.1, bf16[256,128]{1,0:T(8,128)(2,1)} %g_hbm.1, ...), custom_call_target="tpu_custom_call" | custom-call | tf_op jit(solution)/shard_map/pallas_call | solution.py:400
  48.3 0.0 copy-start.1
  48.3 1.5 %copy.14 = bf16[256,128]{1,0:T(8,128)(2,1)} copy(bf16[256,128]{1,0:T(8,128)(2,1)} %get-tuple-element.6) | data formatting | bytes 131072
  49.8 0.0 copy-done.1
  49.8 0.0 copy-start
  49.8 0.6 %copy.15 = bf16[256,128]{1,0:T(8,128)(2,1)} copy(bf16[256,128]{1,0:T(8,128)(2,1)S(1)} %copy-done.1) | data formatting | bytes 131072
  50.4 0.2 copy-done
  50.6 0.6 %copy.16 = bf16[256,128]{1,0:T(8,128)(2,1)} copy(bf16[256,128]{1,0:T(8,128)(2,1)S(1)} %copy-done) | data formatting | bytes 131072
Async XLA Ops:
  48.3 1.5 %copy-start.1 = (bf16[256,128]{1,0:T(8,128)(2,1)S(1)}, bf16[256,128]{1,0:T(8,128)(2,1)}, u32[]{:S(2)}) copy-start(bf16[256,128]{1,0:T(8,128)(2,1)} %get-tuple-element.7) | copy-start | bytes 196612
  49.8 0.9 %copy-start = (bf16[256,128]{1,0:T(8,128)(2,1)S(1)}, bf16[256,128]{1,0:T(8,128)(2,1)}, u32[]{:S(2)}) copy-start(bf16[256,128]{1,0:T(8,128)(2,1)} %get-tuple-element.8) | copy-start | bytes 196612

commit v4 on v3

--- a/solution.py
+++ b/solution.py
@@ -155,14 +155,21 @@
     far = {0: frame_copies(3, 7, ring(2), (0,)), 1: frame_copies(4, 7, ring(-2), (1,))}
     hop[7] = {**far[0], **far[1]}
 
-    def arrive(step):
-        for key, copy in hop[step].items():
-            copy.wait_recv()
-            if step in ONWARD:
-                hop[ONWARD[step]][key].start()
-        if step == 4:
-            for copy in hop[7].values():
-                copy.start()
+    def arrive(steps):
+        keys = {1: ((0, 0), (0, 1), (0, 2), (1, 0), (1, 1), (1, 2))}
+        keys[0] = keys[1][3:] + keys[1][:3]
+        for n in range(6):
+            for step in steps:
+                key = keys[step % 2][n]
+                hop[step][key].wait_recv()
+                if step in ONWARD:
+                    hop[ONWARD[step]][key].start()
+                if step in (3, 4) and n < 3:
+                    waiting.append(key)
+            while waiting:
+                hop[7][waiting.pop(0)].start()
+
+    waiting = []
 
     kv1 = [remote(h, kv.at[1, n], kvs, n, {"slab": mate[1]}) for n, h in enumerate((k_hbm, v_hbm))]
     kv2 = [
@@ -274,14 +281,25 @@
         biases = [[mask_bias(level, 2 * c + h, 2 * c + t) for h in range(2)] for t in range(2)]
         return pair(*frame(qg, stat, s), biases, j, fresh)
 
+    def window(side):
+        @pl.when(odd)
+        def _():
+            for copy in win[side]:
+                copy.wait_recv()
+
+        biases = [
+            [mask_bias(0, 2 * beside[side] + h, 2 * c + t) for h in range(2)] for t in range(2)
+        ]
+        wdq_out[side] = pair(*frame(wqg, wstat, side), biases, 0).astype(BF16)
+        wret[side].start()
+
     key_t(0)
     dq_acc[...] = visit(0, 0, True)
     for copy in kv1:
         copy.wait_recv()
     key_t(1)
     dq_acc[...] += visit(0, 1, True)
-    arrive(1)
-    arrive(2)
+    arrive((1, 2))
     for copy in kv2:
         copy.wait_recv()
     kv3.start()
@@ -292,19 +310,26 @@
     dq_acc[...] += visit(0, 3, True)
 
     def turn(s, carry):
-        for n in range(1, 6):
+        @pl.when(s == 2)
+        def _():
+            arrive((3, 4))
+
+        for n in (5, 6):
             @pl.when(s == n)
             def _():
-                arrive(n + 2)
-
-        @pl.when(s == 4)
-        def _():
-            for side in range(2):
-                @pl.when(has[side] & jnp.logical_not(odd))
-                def _():
-                    for copy in win[side]:
-                        copy.wait_recv()
-                    win_start(1 - side)
+                arrive((n,))
+
+        for side, n in ((1, 3), (0, 4)):
+            @pl.when((s == n) & has[side] & jnp.logical_not(odd))
+            def _():
+                for copy in win[side]:
+                    copy.wait_recv()
+                win_start(1 - side)
+
+        for side in range(2):
+            @pl.when((s == 6) & has[side])
+            def _():
+                window(side)
 
         total = visit(s, 0)
         for j in range(1, 4):
@@ -325,6 +350,7 @@
         kv_out[j, 1] = dv.astype(BF16)
 
     last = jnp.int32(STEPS - 1)
+    arrive((7,))
     total = visit(last, 3)
     pack(3)
     kvret[3].start()
@@ -339,19 +365,6 @@
     kvret[2].start()
 
     for side in range(2):
-        @pl.when(has[side])
-        def _():
-            @pl.when(odd)
-            def _():
-                for copy in win[side]:
-                    copy.wait_recv()
-            biases = [
-                [mask_bias(0, 2 * beside[side] + h, 2 * c + t) for h in range(2)] for t in range(2)
-            ]
-            wdq_out[side] = pair(*frame(wqg, wstat, side), biases, 0).astype(BF16)
-            wret[side].start()
-
-    for side in range(2):
         @pl.when(has[1 - side])
         def _():
             wret[side].wait_recv()
@@ -360,20 +373,14 @@
     for step in range(1, STEPS):
         ret(jnp.int32(step)).wait_recv()
         total = total + dq_in[step].astype(F32)
-    res[0] = (total.T * scale).astype(BF16)
-    stores = [pltpu.make_async_copy(res.at[0], dq_hbm, local_sem.at[0])]
-    stores[0].start()
+    dq_hbm[...] = (total.T * scale).astype(BF16)
 
     for slot in (1, 2):
         kvret[slot].wait_recv()
     dk = dk_acc[0] + kv_in[1, 0].astype(F32) + kv_in[2, 0].astype(F32)
     dv = dv_acc[0] + kv_in[1, 1].astype(F32) + kv_in[2, 1].astype(F32)
-    res[1] = (dk * scale).astype(BF16)
-    res[2] = dv.astype(BF16)
-    for n, out in ((1, dk_hbm), (2, dv_hbm)):
-        copy = pltpu.make_async_copy(res.at[n], out, local_sem.at[n])
-        copy.start()
-        stores.append(copy)
+    dk_hbm[...] = (dk * scale).astype(BF16)
+    dv_hbm[...] = dv.astype(BF16)
 
     for step in range(1, STEPS):
         for copy in hop[step].values():
@@ -387,8 +394,6 @@
             for copy in win[1 - side]:
                 copy.wait_send()
             wret[side].wait_send()
-    for copy in stores:
-        copy.wait()
 
 
 def body(slab_count, space_count, query, key, value, out_saved, grad_out, log_norm, band, frames):
@@ -401,7 +406,7 @@
         functools.partial(kernel, slab_count, space_count, band.shape[0]),
         out_shape=(rows, rows, rows),
         in_specs=[any_spec] * 5 + [vmem, smem, smem],
-        out_specs=[any_spec] * 3,
+        out_specs=[vmem] * 3,
         scratch_shapes=[
             pltpu.VMEM((8, 2, ROWS, DIM), BF16),
             pltpu.VMEM((8, 2, 2, TILE), F32),
@@ -435,9 +440,9 @@
             dma((4,)),
         ],
         compiler_params=pltpu.CompilerParams(
-            collective_id=0, has_side_effects=True, vmem_limit_bytes=63 * 1024 * 1024
+            collective_id=0, has_side_effects=True, vmem_limit_bytes=24 * 1024 * 1024
         ),
-    )(query, key, value, out_saved, grad_out, log_norm, band, frames)
+    )(*[pltpu.with_memory_space_constraint(a, pltpu.HBM) for a in (query, key, value, out_saved, grad_out, log_norm, band, frames)])
 
 
 def solution(mesh):

time: 51.6 us -> 43.4 us (0.84)
  the two profiles are of different devices: /device:TPU:23 before, /device:TPU:65 now
where the time goes in v4:
time: 43.4 us; the launch traced here: 43.2 us
  Pallas kernels  40.6 us (94%)
  local copies, waits for them, and re-layouts  1.89 us (4%)
  between operations  0.64 us (1%)
    pallas_call x1, Pallas kernels, body(): pl.pallas_call(functools.partial(kernel, slab_count, space_count, band.sh...  40.6 us
    unnamed x3, local copies, waits for them, and re-layouts  1.89 us

profile of v4, /device:TPU:65, one launch (start us, length us, event | category | flops | bytes accessed | tf_op | source)
XLA Modules:
  0.0 43.2 jit_solution(13635774156299484908)
XLA Ops:
  0.6 40.6 %shard_map.103 = (bf16[256,128]{1,0:T(8,128)(2,1)S(1)}, bf16[256,128]{1,0:T(8,128)(2,1)S(1)}, bf16[256,128]{1,0:T(8,128)(2,1)S(1)}) custom-call(bf16[256,128]{1,0:T(8,128)(2,1)} %q_hbm.1, bf16[256,128]{1,0:T(8,128)(2,1)} %k_hbm.1, bf16[256,128]{1,0:T(8,128)(2,1)} %v_hbm.1, bf16[256,128]{1,0:T(8,128)(2,1)} %o_hbm.1, bf16[256,128]{1,0:T(8,128)(2,1)} %g_hbm.1, ...), custom_call_target="tpu_custom_call" | custom-call | tf_op jit(solution)/shard_map/pallas_call | solution.py:405
  41.3 0.6 %copy.14 = bf16[256,128]{1,0:T(8,128)(2,1)} copy(bf16[256,128]{1,0:T(8,128)(2,1)S(1)} %get-tuple-element.6) | data formatting | bytes 131072
  41.9 0.6 %copy.15 = bf16[256,128]{1,0:T(8,128)(2,1)} copy(bf16[256,128]{1,0:T(8,128)(2,1)S(1)} %get-tuple-element.7) | data formatting | bytes 131072
  42.5 0.6 %copy.16 = bf16[256,128]{1,0:T(8,128)(2,1)} copy(bf16[256,128]{1,0:T(8,128)(2,1)S(1)} %get-tuple-element.8) | data formatting | bytes 131072

commit v5 on v4

--- a/solution.py
+++ b/solution.py
@@ -41,9 +41,9 @@
     lse_ref,
     band,
     frames,
-    dq_hbm,
-    dk_hbm,
-    dv_hbm,
+    dq_ref,
+    dk_ref,
+    dv_ref,
     qg,
     stat,
     wqg,
@@ -56,11 +56,13 @@
     dq_acc,
     dq_out,
     dq_in,
+    dq_mid,
+    dq7_out,
+    dq7_in,
     wdq_out,
     wdq_in,
     kv_out,
     kv_in,
-    res,
     local_sem,
     fwd_send,
     fwd_recv,
@@ -74,6 +76,7 @@
     wret_recv,
     kvret_send,
     kvret_recv,
+    in_sem,
 ):
     m = lax.axis_index("slab")
     c = lax.axis_index("space")
@@ -195,21 +198,46 @@
     def source(step):
         return ring(jnp.where(step % 2 == 1, -1, 1) * ((step + 1) // 2))
 
-    def ret(step):
+    rets = (ret_send, ret_recv)
+
+    def side_of(step):
+        return jnp.where(step % 2 == 1, -1, 1)
+
+    def ret(step, hops=1):
         return remote(
-            dq_out.at[step], dq_in.at[step], (ret_send, ret_recv), step, {"slab": source(step)}
+            dq_out.at[step], dq_in.at[step], rets, step, {"slab": ring(side_of(step) * hops)}
+        )
+
+    def ret7(tile):
+        return remote(
+            dq7_out.at[tile], dq7_in.at[tile], rets, 7 + tile, {"slab": ring(-2 if tile == 0 else 2)}
         )
 
     kvret = {
-        slot: remote(
-            kv_out.at[slot], kv_in.at[slot], (kvret_send, kvret_recv), slot, {"slab": mate[peer]}
+        (slot, n): remote(
+            kv_out.at[slot, n],
+            kv_in.at[slot, n],
+            (kvret_send, kvret_recv),
+            (slot, n),
+            {"slab": mate[peer]},
         )
         for slot, peer in ((1, 1), (2, 2), (3, 1))
+        for n in range(2)
     }
 
     pl.semaphore_wait(
         barrier, 4 + jnp.where(odd, has[0].astype(jnp.int32) + has[1].astype(jnp.int32), 0)
     )
+
+    for side in range(2):
+        @pl.when(odd & has[side])
+        def _():
+            pl.semaphore_signal(
+                in_sem.at[1 - side],
+                inc=1,
+                device_id={"space": beside[side]},
+                device_id_type=MESH,
+            )
 
     for key in ((0, 0), (0, 1), (1, 0), (1, 1)):
         hop[1][key].start()
@@ -282,10 +310,8 @@
         return pair(*frame(qg, stat, s), biases, j, fresh)
 
     def window(side):
-        @pl.when(odd)
-        def _():
-            for copy in win[side]:
-                copy.wait_recv()
+        for copy in win[side]:
+            copy.wait_recv()
 
         biases = [
             [mask_bias(0, 2 * beside[side] + h, 2 * c + t) for h in range(2)] for t in range(2)
@@ -293,13 +319,56 @@
         wdq_out[side] = pair(*frame(wqg, wstat, side), biases, 0).astype(BF16)
         wret[side].start()
 
+    def visit_all(s):
+        q, g, lse, delta = frame(qg, stat, s)
+        keys = jnp.concatenate([kv[j, 0] for j in range(4)], axis=0)
+        values = jnp.concatenate([kv[j, 1] for j in range(4)], axis=0)
+        scores = dot_nt(keys, q)
+        dprobs = dot_nt(values, g)
+        probs, dscores = [], []
+        for j in range(4):
+            level = level_between(source(s), mate[j])
+            for t in range(2):
+                bias = [mask_bias(level, 2 * c + h, 2 * c + t) for h in range(2)]
+                shift = lse + jnp.where(lane < TILE, bias[0], bias[1])
+                at = (2 * j + t) * TILE
+                prob = jnp.exp2(scores[at : at + TILE] * (scale * LOG2E) - shift)
+                probs.append(prob.astype(BF16))
+                dscores.append((prob * (dprobs[at : at + TILE] - delta)).astype(BF16))
+        prob = jnp.concatenate(probs, axis=0)
+        dscore = jnp.concatenate(dscores, axis=0)
+        dv = dot_nn(prob, g)
+        dk = dot_nn(dscore, q)
+        for j in range(4):
+            dv_acc[j] += dv[j * ROWS : (j + 1) * ROWS]
+            dk_acc[j] += dk[j * ROWS : (j + 1) * ROWS]
+        kt_all = jnp.concatenate([kt[j] for j in range(4)], axis=1)
+        return dot_nn(kt_all, dscore)
+
+    even = jnp.logical_not(odd)
+    far_left = even & has[0] & (c % (space_count // 2) == 0)
+
+    def answer(side):
+        pl.semaphore_wait(in_sem.at[side], 1)
+        win_start(1 - side)
+
     key_t(0)
     dq_acc[...] = visit(0, 0, True)
+
+    @pl.when(even & has[0] & (c % (space_count // 2) != 0))
+    def _():
+        answer(0)
+
     for copy in kv1:
         copy.wait_recv()
     key_t(1)
     dq_acc[...] += visit(0, 1, True)
     arrive((1, 2))
+
+    @pl.when(even & has[1])
+    def _():
+        answer(1)
+
     for copy in kv2:
         copy.wait_recv()
     kv3.start()
@@ -309,60 +378,73 @@
     key_t(3)
     dq_acc[...] += visit(0, 3, True)
 
-    def turn(s, carry):
+    def turn(turn_index, carry):
+        s = turn_index
         @pl.when(s == 2)
         def _():
             arrive((3, 4))
 
-        for n in (5, 6):
-            @pl.when(s == n)
-            def _():
-                arrive((n,))
-
-        for side, n in ((1, 3), (0, 4)):
-            @pl.when((s == n) & has[side] & jnp.logical_not(odd))
-            def _():
-                for copy in win[side]:
-                    copy.wait_recv()
-                win_start(1 - side)
+        @pl.when((s == 4) & far_left)
+        def _():
+            answer(0)
 
         for side in range(2):
             @pl.when((s == 6) & has[side])
             def _():
                 window(side)
 
-        total = visit(s, 0)
-        for j in range(1, 4):
-            total = total + visit(s, j)
-        dq_out[s] = total.astype(BF16)
-        ret(s).start()
+        for n in (5, 6, 7):
+            @pl.when(s == n)
+            def _():
+                arrive((n,))
+
+        total = visit_all(s)
+        middle = (s == 3) | (s == 4)
+
+        @pl.when(middle)
+        def _():
+            dq_mid[s - 3] = total
+
+        @pl.when(s == 7)
+        def _():
+            for tile in range(2):
+                dq7_out[tile] = total[:, tile * TILE : (tile + 1) * TILE].astype(BF16)
+                ret7(tile).start()
+
+        @pl.when(jnp.logical_not(middle | (s == 7)))
+        def _():
+            dq_out[s] = total.astype(BF16)
+            ret(s).start()
+
         return carry
 
-    lax.fori_loop(1, STEPS - 1, turn, 0)
-
-    def pack(j, extra=None):
-        dk = dk_acc[j]
-        dv = dv_acc[j]
-        if extra is not None:
-            dk = dk + kv_in[extra, 0].astype(F32)
-            dv = dv + kv_in[extra, 1].astype(F32)
-        kv_out[j, 0] = dk.astype(BF16)
-        kv_out[j, 1] = dv.astype(BF16)
-
-    last = jnp.int32(STEPS - 1)
-    arrive((7,))
-    total = visit(last, 3)
-    pack(3)
-    kvret[3].start()
-    for j in (2, 1, 0):
-        total = total + visit(last, j)
-    dq_out[last] = total.astype(BF16)
-    ret(last).start()
-    pack(1)
-    kvret[1].start()
-    kvret[3].wait_recv()
-    pack(2, 3)
-    kvret[2].start()
+    lax.fori_loop(1, STEPS, turn, 0)
+
+    sums = (dk_acc, dv_acc)
+
+    def give(j, extra=None):
+        for n in range(2):
+            part = sums[n][j]
+            if extra is not None:
+                kvret[extra, n].wait_recv()
+                part = part + kv_in[extra, n].astype(F32)
+            kv_out[j, n] = part.astype(BF16)
+            kvret[j, n].start()
+
+    give(3)
+    give(1)
+    give(2, 3)
+
+    for n in range(2):
+        ret(jnp.int32(5 + n)).wait_recv()
+        part = dq_mid[n] + dq_in[5 + n].astype(F32)
+        ret7(n).wait_recv()
+        far_part = dq7_in[n].astype(F32)
+        halves = [part[:, :TILE], part[:, TILE:]]
+        halves[n] = halves[n] + far_part
+        for tile in range(2):
+            dq_out[3 + n, :, tile * TILE : (tile + 1) * TILE] = halves[tile].astype(BF16)
+        ret(jnp.int32(3 + n), 2).start()
 
     for side in range(2):
         @pl.when(has[1 - side])
@@ -370,22 +452,25 @@
             wret[side].wait_recv()
             dq_acc[...] += wdq_in[side].astype(F32)
     total = dq_acc[...]
-    for step in range(1, STEPS):
-        ret(jnp.int32(step)).wait_recv()
+    for step in range(1, 5):
+        ret(jnp.int32(step), (step + 1) // 2).wait_recv()
         total = total + dq_in[step].astype(F32)
-    dq_hbm[...] = (total.T * scale).astype(BF16)
-
-    for slot in (1, 2):
-        kvret[slot].wait_recv()
-    dk = dk_acc[0] + kv_in[1, 0].astype(F32) + kv_in[2, 0].astype(F32)
-    dv = dv_acc[0] + kv_in[1, 1].astype(F32) + kv_in[2, 1].astype(F32)
-    dk_hbm[...] = (dk * scale).astype(BF16)
-    dv_hbm[...] = dv.astype(BF16)
+    dq_ref[...] = (total.T * scale).astype(BF16)
+
+    for n, out in ((0, dk_ref), (1, dv_ref)):
+        part = sums[n][0]
+        for slot in (1, 2):
+            kvret[slot, n].wait_recv()
+            part = part + kv_in[slot, n].astype(F32)
+        out[...] = (part * scale if n == 0 else part).astype(BF16)
 
     for step in range(1, STEPS):
         for copy in hop[step].values():
             copy.wait_send()
-        ret(jnp.int32(step)).wait_send()
+        if step < 7:
+            ret(jnp.int32(step), 2 if step in (3, 4) else 1).wait_send()
+    for tile in range(2):
+        ret7(tile).wait_send()
     for copy in kv1 + kv2 + [kv3] + list(kvret.values()):
         copy.wait_send()
     for side in range(2):
@@ -420,11 +505,13 @@
             pltpu.VMEM((DIM, ROWS), F32),
             pltpu.VMEM((8, DIM, ROWS), BF16),
             pltpu.VMEM((8, DIM, ROWS), BF16),
+            pltpu.VMEM((2, DIM, ROWS), F32),
+            pltpu.VMEM((2, DIM, TILE), BF16),
+            pltpu.VMEM((2, DIM, TILE), BF16),
             pltpu.VMEM((2, DIM, ROWS), BF16),
             pltpu.VMEM((2, DIM, ROWS), BF16),
             pltpu.VMEM((4, 2, ROWS, DIM), BF16),
             pltpu.VMEM((4, 2, ROWS, DIM), BF16),
-            pltpu.VMEM((3, ROWS, DIM), BF16),
             dma((8,)),
             dma((8, 2, 3)),
             dma((8, 2, 3)),
@@ -432,12 +519,13 @@
             dma((2, 3)),
             dma((5,)),
             dma((5,)),
-            dma((8,)),
-            dma((8,)),
+            dma((9,)),
+            dma((9,)),
             dma((2,)),
             dma((2,)),
-            dma((4,)),
-            dma((4,)),
+            dma((4, 2)),
+            dma((4, 2)),
+            pltpu.SemaphoreType.REGULAR((2,)),
         ],
         compiler_params=pltpu.CompilerParams(
             collective_id=0, has_side_effects=True, vmem_limit_bytes=24 * 1024 * 1024

time: 43.4 us -> 42.3 us (0.975)
  the two profiles are of different devices: /device:TPU:65 before, /device:TPU:192 now
where the time goes in v5:
time: 42.3 us; the launch traced here: 42 us
  Pallas kernels  39.5 us (93%)
  local copies, waits for them, and re-layouts  1.89 us (4%)
  between operations  0.64 us (2%)
    pallas_call x1, Pallas kernels, body(): pl.pallas_call(functools.partial(kernel, slab_count, space_count, band.sh...  39.5 us
    unnamed x3, local copies, waits for them, and re-layouts  1.89 us

profile of v5, /device:TPU:192, one launch (start us, length us, event | category | flops | bytes accessed | tf_op | source)
XLA Modules:
  0.0 42.0 jit_solution(1024584175746572477)
XLA Ops:
  0.6 39.5 %shard_map.103 = (bf16[256,128]{1,0:T(8,128)(2,1)S(1)}, bf16[256,128]{1,0:T(8,128)(2,1)S(1)}, bf16[256,128]{1,0:T(8,128)(2,1)S(1)}) custom-call(bf16[256,128]{1,0:T(8,128)(2,1)} %q_hbm.1, bf16[256,128]{1,0:T(8,128)(2,1)} %k_hbm.1, bf16[256,128]{1,0:T(8,128)(2,1)} %v_hbm.1, bf16[256,128]{1,0:T(8,128)(2,1)} %o_hbm.1, bf16[256,128]{1,0:T(8,128)(2,1)} %g_hbm.1, ...), custom_call_target="tpu_custom_call" | custom-call | tf_op jit(solution)/shard_map/pallas_call | solution.py:490
  40.1 0.6 %copy.14 = bf16[256,128]{1,0:T(8,128)(2,1)} copy(bf16[256,128]{1,0:T(8,128)(2,1)S(1)} %get-tuple-element.6) | data formatting | bytes 131072
  40.8 0.6 %copy.15 = bf16[256,128]{1,0:T(8,128)(2,1)} copy(bf16[256,128]{1,0:T(8,128)(2,1)S(1)} %get-tuple-element.7) | data formatting | bytes 131072
  41.4 0.6 %copy.16 = bf16[256,128]{1,0:T(8,128)(2,1)} copy(bf16[256,128]{1,0:T(8,128)(2,1)S(1)} %get-tuple-element.8) | data formatting | bytes 131072

commit v6 on v5

--- a/solution.py
+++ b/solution.py
@@ -41,9 +41,7 @@
     lse_ref,
     band,
     frames,
-    dq_ref,
-    dk_ref,
-    dv_ref,
+    out_ref,
     qg,
     stat,
     wqg,
@@ -388,10 +386,13 @@
         def _():
             answer(0)
 
-        for side in range(2):
-            @pl.when((s == 6) & has[side])
-            def _():
-                window(side)
+        @pl.when(has[0] & (s == jnp.where(c % (space_count // 2) == 0, 6, 4)))
+        def _():
+            window(0)
+
+        @pl.when(has[1] & (s == 5))
+        def _():
+            window(1)
 
         for n in (5, 6, 7):
             @pl.when(s == n)
@@ -455,14 +456,14 @@
     for step in range(1, 5):
         ret(jnp.int32(step), (step + 1) // 2).wait_recv()
         total = total + dq_in[step].astype(F32)
-    dq_ref[...] = (total.T * scale).astype(BF16)
-
-    for n, out in ((0, dk_ref), (1, dv_ref)):
+    out_ref[:ROWS, :] = (total.T * scale).astype(BF16)
+
+    for n in range(2):
         part = sums[n][0]
         for slot in (1, 2):
             kvret[slot, n].wait_recv()
             part = part + kv_in[slot, n].astype(F32)
-        out[...] = (part * scale if n == 0 else part).astype(BF16)
+        out_ref[(n + 1) * ROWS : (n + 2) * ROWS, :] = (part * scale if n == 0 else part).astype(BF16)
 
     for step in range(1, STEPS):
         for copy in hop[step].values():
@@ -485,13 +486,12 @@
     any_spec = pl.BlockSpec(memory_space=pl.ANY)
     smem = pl.BlockSpec(memory_space=pltpu.SMEM)
     vmem = pl.BlockSpec(memory_space=pltpu.VMEM)
-    rows = jax.ShapeDtypeStruct((ROWS, DIM), BF16)
     dma = pltpu.SemaphoreType.DMA
-    return pl.pallas_call(
+    grads = pl.pallas_call(
         functools.partial(kernel, slab_count, space_count, band.shape[0]),
-        out_shape=(rows, rows, rows),
+        out_shape=jax.ShapeDtypeStruct((3 * ROWS, DIM), BF16),
         in_specs=[any_spec] * 5 + [vmem, smem, smem],
-        out_specs=[vmem] * 3,
+        out_specs=vmem,
         scratch_shapes=[
             pltpu.VMEM((8, 2, ROWS, DIM), BF16),
             pltpu.VMEM((8, 2, 2, TILE), F32),
@@ -532,6 +532,8 @@
         ),
     )(*[pltpu.with_memory_space_constraint(a, pltpu.HBM) for a in (query, key, value, out_saved, grad_out, log_norm, band, frames)])
 
+    return tuple(grads[n * ROWS : (n + 1) * ROWS] for n in range(3))
+
 
 def solution(mesh):
     rows = P(("slab", "space"), None)

time: 42.3 us -> 40.4 us (0.955)
  the two profiles are of different devices: /device:TPU:192 before, /device:TPU:194 now
where the time goes in v6:
time: 40.4 us; the launch traced here: 40.1 us
  Pallas kernels  38.8 us (96%)
  local copies, waits for them, and re-layouts  0.68 us (2%)
  between operations  0.64 us (2%)
    pallas_call x1, Pallas kernels, body(): pl.pallas_call(functools.partial(kernel, slab_count, space_count, band.sh...  38.8 us

profile of v6, /device:TPU:194, one launch (start us, length us, event | category | flops | bytes accessed | tf_op | source)
XLA Modules:
  0.0 40.1 jit_solution(9205858297629253930)
XLA Ops:
  0.6 38.8 %shard_map.103 = bf16[768,128]{1,0:T(8,128)(2,1)S(1)} custom-call(bf16[256,128]{1,0:T(8,128)(2,1)} %q_hbm.1, bf16[256,128]{1,0:T(8,128)(2,1)} %k_hbm.1, bf16[256,128]{1,0:T(8,128)(2,1)} %v_hbm.1, bf16[256,128]{1,0:T(8,128)(2,1)} %o_hbm.1, bf16[256,128]{1,0:T(8,128)(2,1)} %g_hbm.1, f32[1,256]{1,0:T(1,128)} %lse_ref.1, s32[6,32,32]{2,1,0:T(8,128)} %band.1, ...), custom_call_target="tpu_custom_call" | custom-call | tf_op jit(solution)/shard_map/pallas_call | solution.py:490
  39.4 0.7 %fusion = (bf16[256,128]{1,0:T(8,128)(2,1)}, bf16[256,128]{1,0:T(8,128)(2,1)}, bf16[256,128]{1,0:T(8,128)(2,1)}) fusion(bf16[768,128]{1,0:T(8,128)(2,1)S(1)} %shard_map.103), kind=kLoop, calls=%fused_computation | loop fusion | bytes 393216 | tf_op jit(solution)/shard_map/slice | solution.py:535

commit v7 on v6

--- a/solution.py
+++ b/solution.py
@@ -156,21 +156,20 @@
     far = {0: frame_copies(3, 7, ring(2), (0,)), 1: frame_copies(4, 7, ring(-2), (1,))}
     hop[7] = {**far[0], **far[1]}
 
-    def arrive(steps):
+    def arrive(steps, numbers=range(6)):
         keys = {1: ((0, 0), (0, 1), (0, 2), (1, 0), (1, 1), (1, 2))}
         keys[0] = keys[1][3:] + keys[1][:3]
-        for n in range(6):
-            for step in steps:
-                key = keys[step % 2][n]
+        for n in numbers:
+            pieces = [(step, keys[step % 2][n]) for step in steps]
+            for step, key in pieces:
                 hop[step][key].wait_recv()
-                if step in ONWARD:
+                if step in ONWARD and (step not in (3, 4) or n >= 3):
                     hop[ONWARD[step]][key].start()
-                if step in (3, 4) and n < 3:
-                    waiting.append(key)
-            while waiting:
-                hop[7][waiting.pop(0)].start()
-
-    waiting = []
+            if steps == (3, 4) and n < 3:
+                for _, key in pieces:
+                    hop[7][key].start()
+                for step, key in pieces:
+                    hop[ONWARD[step]][key].start()
 
     kv1 = [remote(h, kv.at[1, n], kvs, n, {"slab": mate[1]}) for n, h in enumerate((k_hbm, v_hbm))]
     kv2 = [
@@ -377,10 +376,11 @@
     dq_acc[...] += visit(0, 3, True)
 
     def turn(turn_index, carry):
-        s = turn_index
-        @pl.when(s == 2)
-        def _():
-            arrive((3, 4))
+        s = jnp.where(turn_index < 5, turn_index, 5 + (turn_index - 3) % 3)
+        for n in (1, 2):
+            @pl.when(s == n)
+            def _():
+                arrive((3, 4), range(3 * n - 3, 3 * n))
 
         @pl.when((s == 4) & far_left)
         def _():

time: 40.4 us -> 38.8 us (0.960)
  the two profiles are of different devices: /device:TPU:194 before, /device:TPU:192 now
where the time goes in v7:
time: 38.8 us; the launch traced here: 38.5 us
  Pallas kernels  37.2 us (96%)
  local copies, waits for them, and re-layouts  0.68 us (2%)
  between operations  0.64 us (2%)
    pallas_call x1, Pallas kernels, body(): pl.pallas_call(functools.partial(kernel, slab_count, space_count, band.sh...  37.2 us

profile of v7, /device:TPU:192, one launch (start us, length us, event | category | flops | bytes accessed | tf_op | source)
XLA Modules:
  0.0 38.5 jit_solution(3498899081194966124)
XLA Ops:
  0.6 37.2 %shard_map.103 = bf16[768,128]{1,0:T(8,128)(2,1)S(1)} custom-call(bf16[256,128]{1,0:T(8,128)(2,1)} %q_hbm.1, bf16[256,128]{1,0:T(8,128)(2,1)} %k_hbm.1, bf16[256,128]{1,0:T(8,128)(2,1)} %v_hbm.1, bf16[256,128]{1,0:T(8,128)(2,1)} %o_hbm.1, bf16[256,128]{1,0:T(8,128)(2,1)} %g_hbm.1, f32[1,256]{1,0:T(1,128)} %lse_ref.1, s32[6,32,32]{2,1,0:T(8,128)} %band.1, ...), custom_call_target="tpu_custom_call" | custom-call | tf_op jit(solution)/shard_map/pallas_call | solution.py:490
  37.9 0.7 %fusion = (bf16[256,128]{1,0:T(8,128)(2,1)}, bf16[256,128]{1,0:T(8,128)(2,1)}, bf16[256,128]{1,0:T(8,128)(2,1)}) fusion(bf16[768,128]{1,0:T(8,128)(2,1)S(1)} %shard_map.103), kind=kLoop, calls=%fused_computation | loop fusion | bytes 393216 | tf_op jit(solution)/shard_map/slice | solution.py:535

commit v8 on v7

--- a/solution.py
+++ b/solution.py
@@ -156,10 +156,10 @@
     far = {0: frame_copies(3, 7, ring(2), (0,)), 1: frame_copies(4, 7, ring(-2), (1,))}
     hop[7] = {**far[0], **far[1]}
 
-    def arrive(steps, numbers=range(6)):
+    def arrive(steps):
         keys = {1: ((0, 0), (0, 1), (0, 2), (1, 0), (1, 1), (1, 2))}
         keys[0] = keys[1][3:] + keys[1][:3]
-        for n in numbers:
+        for n in range(6):
             pieces = [(step, keys[step % 2][n]) for step in steps]
             for step, key in pieces:
                 hop[step][key].wait_recv()
@@ -377,10 +377,9 @@
 
     def turn(turn_index, carry):
         s = jnp.where(turn_index < 5, turn_index, 5 + (turn_index - 3) % 3)
-        for n in (1, 2):
-            @pl.when(s == n)
-            def _():
-                arrive((3, 4), range(3 * n - 3, 3 * n))
+        @pl.when(s == 1)
+        def _():
+            arrive((3, 4))
 
         @pl.when((s == 4) & far_left)
         def _():

time: 38.8 us -> 38.3 us (0.987)
  the two profiles are of different devices: /device:TPU:192 before, /device:TPU:194 now
where the time goes in v8:
time: 38.3 us; the launch traced here: 38.1 us
  Pallas kernels  36.8 us (96%)
  local copies, waits for them, and re-layouts  0.68 us (2%)
  between operations  0.64 us (2%)
    pallas_call x1, Pallas kernels, body(): pl.pallas_call(functools.partial(kernel, slab_count, space_count, band.sh...  36.8 us

profile of v8, /device:TPU:194, one launch (start us, length us, event | category | flops | bytes accessed | tf_op | source)
XLA Modules:
  0.0 38.1 jit_solution(9269753298448672629)
XLA Ops:
  0.6 36.8 %shard_map.103 = bf16[768,128]{1,0:T(8,128)(2,1)S(1)} custom-call(bf16[256,128]{1,0:T(8,128)(2,1)} %q_hbm.1, bf16[256,128]{1,0:T(8,128)(2,1)} %k_hbm.1, bf16[256,128]{1,0:T(8,128)(2,1)} %v_hbm.1, bf16[256,128]{1,0:T(8,128)(2,1)} %o_hbm.1, bf16[256,128]{1,0:T(8,128)(2,1)} %g_hbm.1, f32[1,256]{1,0:T(1,128)} %lse_ref.1, s32[6,32,32]{2,1,0:T(8,128)} %band.1, ...), custom_call_target="tpu_custom_call" | custom-call | tf_op jit(solution)/shard_map/pallas_call | solution.py:489
  37.4 0.7 %fusion = (bf16[256,128]{1,0:T(8,128)(2,1)}, bf16[256,128]{1,0:T(8,128)(2,1)}, bf16[256,128]{1,0:T(8,128)(2,1)}) fusion(bf16[768,128]{1,0:T(8,128)(2,1)S(1)} %shard_map.103), kind=kLoop, calls=%fused_computation | loop fusion | bytes 393216 | tf_op jit(solution)/shard_map/slice | solution.py:534
